TPU v7x, 512 devices: a whole 4x4x16 slice. The times are simulated.
512 devices in a mesh: channel: 16 (over z_hi, x), tm: 4 (over y), beam: 8 (over z_lo, core).
Axes of the slice: x: 4, y: 4, z: 16 (z_hi: 4, z_lo: 4; z = z_hi * 4 + z_lo), core: 2. Of those that a mesh axis runs over, the one named last changes fastest.
Arguments:
- voltages: bfloat16 [2, 2048, 64, 1024], P(None, ('beam', 'channel'), None, 'tm'), may hold values from -6 to 6
- positions: int32 [2048], replicated, may hold values from 0 to 1023
- delays: int32 [128, 1024], P(None, 'channel'), may hold values from 0 to 63
Outputs:
- intensity: float32 [1024, 64, 1024], P(('beam', 'tm'), 'channel')
- dedispersed: float32 [1024, 128, 64], P(('beam', 'tm'), 'channel')
Inputs may be any that keep to these rules, and one draw needn't show every extreme that they name: `positions`: place on a grid of 4 cylinders by 256 places along each.
All inputs are finite; a program needn't handle non-finite values.
Results may differ from a plain program's by a relative error of at most 0.0071.
Values may be sent and summed in bfloat16 or wider, within the bound.
A program may use at most 64 MiB of HBM per device.

v0:
```python
import math

import jax
import jax.numpy as jnp
from jax import lax
from jax.sharding import Mesh
from jax.sharding import PartitionSpec as P

BEAMS = 1024
UPCH = 16
TAPS = 8
FINE = 1024
CHANNEL_BEAM = ("channel", "beam_0", "beam_1")
BEAM = ("beam_0", "beam_1")
BEAM_CHANNEL = ("beam_0", "beam_1", "channel")
BEAM_TM = ("beam_0", "beam_1", "tm")


TWO_PI = 2.0 * math.pi
HIGHEST = lax.Precision.HIGHEST


def split_up(array, dim, peers):
    dims = array.shape
    parts = array.reshape(*dims[:dim], peers, dims[dim] // peers, *dims[dim + 1 :])
    return jnp.moveaxis(parts, dim, 0)


def laid_out(parts, dim):
    parts = jnp.moveaxis(parts, 0, dim)
    dims = parts.shape
    return parts.reshape(*dims[:dim], dims[dim] * dims[dim + 1], *dims[dim + 2 :])


def exchange_both(array, axis, axes, splits, concats):
    sizes = [lax.axis_size(a) for a in axes]
    parts = split_up(array, splits[0], sizes[0])
    parts = jnp.moveaxis(split_up(parts, splits[1] + 1, sizes[1]), 0, 1)
    inside = parts.shape[2:]
    parts = parts.reshape(-1, *inside)
    parts = lax.all_to_all(parts, axis, split_axis=0, concat_axis=0, tiled=True)
    parts = laid_out(parts.reshape(*sizes, *inside), concats[0] + 1)
    return laid_out(parts, concats[1])


def moved_by_axis(parts, axes, sequence):
    inside = parts.shape[1:]
    out = parts.reshape(*(lax.axis_size(a) for a in axes), *inside)
    for k in sequence:
        out = lax.all_to_all(out, axes[k], k, k, tiled=True)
    return out.reshape(-1, *inside)


def two_step_exchange(array, groups, sequence, split_dim, concat_dim):
    peers = lax.axis_size(groups[0]) * lax.axis_size(groups[1])
    parts = split_up(array, split_dim, peers)
    return laid_out(moved_by_axis(parts, groups, sequence), concat_dim)


def from_behind(value, axis, steps):
    count = lax.axis_size(axis)
    first, last = (max(0, -steps), min(count, count - steps))
    return lax.ppermute(value, axis, [(source, source + steps) for source in range(first, last)])


def for_sending(array):

    def short(part):
        return part.astype(jnp.bfloat16) if part.dtype == jnp.float32 else part

    return jax.tree.map(short, array)


def sent_and_summed(array, axis, dim):
    parts = split_up(array, dim, lax.axis_size(axis))
    arrived = lax.all_to_all(parts, axis, split_axis=0, concat_axis=0, tiled=True)
    return arrived.astype(jnp.float32).sum(axis=0)


def window_table(tap_count, upch_factor):
    length = tap_count * upch_factor
    sample_index = jnp.arange(length).astype(jnp.float32)
    taper = jnp.sinc((sample_index - (length - 1) / 2.0) / upch_factor) * (
        0.5 - 0.5 * jnp.cos(TWO_PI * (sample_index + 0.5) / length)
    )
    taper = taper / jnp.sqrt(jnp.sum(taper * taper))
    return taper.reshape(tap_count, upch_factor)


def steering(positions, beam_start, item_count, places, feed_count):
    beam_ids = beam_start + jnp.arange(item_count)
    beam_east = beam_ids // places
    beam_north = beam_ids % places
    cylinder = positions // places
    along_row = positions % places
    coarse = beam_east[:, None] * cylinder[None, :] % 4
    north_turns = beam_north[:, None] * along_row[None, :] % places
    angles = TWO_PI * (coarse.astype(jnp.float32) / 4.0 + north_turns.astype(jnp.float32) / places)
    norm_scale = 1.0 / math.sqrt(feed_count)
    w_real = (jnp.cos(angles) * norm_scale).astype(jnp.bfloat16)
    w_imag = (-jnp.sin(angles) * norm_scale).astype(jnp.bfloat16)
    top_half = jnp.concatenate([w_real, -w_imag], axis=1)
    low_half = jnp.concatenate([w_imag, w_real], axis=1)
    return jnp.concatenate([top_half, low_half], axis=0)


def upchannel_matrix(upch_factor):
    sample_index = jnp.arange(128)
    frame_part = sample_index // upch_factor
    inner = sample_index % upch_factor
    same_frame = frame_part[:, None] == frame_part[None, :]
    angles = (inner[:, None] * inner[None, :] % upch_factor).astype(jnp.float32) * (
        TWO_PI / upch_factor
    )
    cos_part = jnp.where(same_frame, jnp.cos(angles), 0.0)
    sin_part = jnp.where(same_frame, -jnp.sin(angles), 0.0)
    top_half = jnp.concatenate([cos_part, sin_part], axis=1)
    low_half = jnp.concatenate([-sin_part, cos_part], axis=1)
    return jnp.concatenate([top_half, low_half], axis=0)


def per_device(voltages, positions, delays):
    places = BEAMS // 4
    turned = exchange_both(voltages, CHANNEL_BEAM, ("channel", BEAM), (2, 3), (1, 1))
    feed_count = turned.shape[1]
    chan_count = turned.shape[2]
    short_count = turned.shape[3]
    stacked = turned.reshape(2 * feed_count, chan_count * short_count)
    block_size = min(128, BEAMS)
    block_count = BEAMS // block_size

    def form_block(beam_start):
        weights = steering(positions, beam_start, block_size, places, feed_count)
        return jnp.dot(weights, stacked, preferred_element_type=jnp.float32).astype(jnp.bfloat16)

    formed = lax.map(form_block, jnp.arange(block_count) * block_size)
    formed = formed.reshape(block_count, 2, block_size, chan_count, short_count)
    formed = jnp.transpose(formed, (1, 0, 2, 3, 4)).reshape(2, BEAMS, chan_count, short_count)
    beams = two_step_exchange(formed, ("beam_0", "beam_1"), (1, 0), 1, 3)
    beam_count = beams.shape[1]
    chan_count = beams.shape[2]
    sample_count = beams.shape[3]
    rim_width = (TAPS - 1) * UPCH
    previous = from_behind(beams[:, :, :, sample_count - rim_width :], "tm", 1)
    extended = jnp.concatenate([previous, beams], axis=3)
    window = window_table(TAPS, UPCH)
    filtered = jnp.zeros(beams.shape, jnp.float32)
    for tap_index in range(TAPS):
        filtered = filtered + extended[
            :, :, :, tap_index * UPCH : tap_index * UPCH + sample_count
        ] * jnp.tile(window[tap_index], sample_count // UPCH)
    row_count = beam_count * chan_count
    tile_count = sample_count // 128
    halves = filtered.reshape(2, row_count, tile_count, 128)
    paired = jnp.concatenate([halves[0], halves[1]], axis=2)
    spectra = jnp.dot(paired, upchannel_matrix(UPCH), precision=HIGHEST)
    real_part = spectra[:, :, :128]
    imag_part = spectra[:, :, 128:]
    power_grid = (real_part * real_part + imag_part * imag_part).reshape(
        beam_count, chan_count, sample_count
    )
    intensity = lax.all_to_all(
        for_sending(power_grid), "tm", split_axis=0, concat_axis=2, tiled=True
    ).astype(power_grid.dtype)
    beam_local = intensity.shape[0]
    frame_count = intensity.shape[2] // UPCH
    frame_grid = intensity.reshape(beam_local, chan_count, frame_count, UPCH)
    centred = frame_grid - jnp.mean(frame_grid, axis=2, keepdims=True)
    frame_index = jnp.arange(frame_count)
    angles = (frame_index[:, None] * frame_index[None, :] % frame_count).astype(jnp.float32) * (
        TWO_PI / frame_count
    )
    forward = jnp.concatenate([jnp.cos(angles), -jnp.sin(angles)], axis=1)
    fine_local = chan_count * UPCH
    transformed = jnp.einsum("bcnk,nw->wbck", centred, forward, precision=HIGHEST)
    transformed = transformed.reshape(2, frame_count, beam_local, fine_local)
    trial_count = delays.shape[0]
    delay_cols = jnp.transpose(delays)
    bin_block = min(16, frame_count)

    def dedisperse(bin_start):
        frequency = bin_start + jnp.arange(bin_block)
        angle_grid = (frequency[:, None, None] * delay_cols[None, :, :] % frame_count).astype(
            jnp.float32
        ) * (TWO_PI / frame_count)
        cos_table = jnp.cos(angle_grid)
        sin_table = jnp.sin(angle_grid)
        table = jnp.concatenate(
            [
                jnp.concatenate([cos_table, -sin_table], axis=2),
                jnp.concatenate([sin_table, cos_table], axis=2),
            ],
            axis=1,
        )
        left_real = lax.dynamic_slice_in_dim(transformed[0], bin_start, bin_block, 0)
        left_imag = lax.dynamic_slice_in_dim(transformed[1], bin_start, bin_block, 0)
        left_side = jnp.concatenate([left_real, left_imag], axis=2)
        return jnp.einsum("vbk,vkd->vbd", left_side, table, precision=HIGHEST)

    trials = lax.map(dedisperse, jnp.arange(frame_count // bin_block) * bin_block)
    trials = trials.reshape(frame_count, beam_local, 2, trial_count)
    inverse = jnp.stack([jnp.cos(angles), -jnp.sin(angles)]) / (frame_count * math.sqrt(FINE))
    partial_series = jnp.einsum("vbrd,rvn->bdn", trials, inverse, precision=HIGHEST)
    dedispersed = sent_and_summed(partial_series.astype(jnp.bfloat16), "channel", 1)
    return (intensity, dedispersed)


def solution(mesh):
    finer = Mesh(
        mesh.devices.reshape(mesh.shape["channel"], mesh.shape["tm"], 4, 2),
        ("channel", "tm", "beam_0", "beam_1"),
    )
    return jax.shard_map(
        per_device,
        mesh=finer,
        in_specs=(P(None, BEAM_CHANNEL, None, "tm"), P(), P(None, "channel")),
        out_specs=(P(BEAM_TM, "channel", None), P(BEAM_TM, "channel", None)),
        check_vma=False,
    )
```

profile of v0, /device:TPU:1, one launch (start us, length us, event | category | flops | bytes accessed | tf_op | source)
XLA Modules:
  0.0 332.6 jit_solution(17851094328855923197)
XLA Ops:
  0.6 1.3 reshape.282
  2.0 0.9 copy.145
  2.9 3.4 %reshape.283 = bf16[16,2,16,4,8,32]{5,4,2,3,1,0:T(8,128)(2,1)} reshape(bf16[16,2,16,4,256]{4,2,3,1,0:T(8,128)(2,1)S(1)} %bitcast.103) | data formatting | bytes 2097152 | tf_op jit(solution)/shard_map/reshape | solution.py:25
  6.2 5.4 %copy.110 = bf16[16,8,2,16,4,32]{5,3,4,2,1,0:T(8,128)(2,1)} copy(bf16[16,8,2,16,4,32]{5,1,3,4,2,0:T(8,128)(2,1)} %bitcast.98) | data formatting | bytes 2097152 | tf_op jit(solution)/shard_map/transpose;transpose | solution.py:38
  11.6 7.3 %reshape.302 = bf16[128,2,2048]{2,1,0:T(2,128)(2,1)} reshape(bf16[128,2,4,16,32]{4,3,2,1,0:T(8,128)(2,1)} %bitcast.99) | data formatting | bytes 2097152
  18.9 20.5 %all-to-all-start = ((bf16[128,2,2048]{2,1,0:T(2,128)(2,1)}), bf16[128,2,2048]{2,1,0:T(2,128)(2,1)S(1)}, u32[]{:S(2)}, u32[]{:S(2)}) async-start(bf16[128,2,2048]{2,1,0:T(2,128)(2,1)} %reshape.302), calls=%async_computation | async-start | bytes 2097152 | tf_op jit(solution)/shard_map/all_to_all | solution.py:41
  39.5 55.9 %all-to-all-done = bf16[128,2,2048]{2,1,0:T(2,128)(2,1)S(1)} async-done(((bf16[128,2,2048]{2,1,0:T(2,128)(2,1)}), bf16[128,2,2048]{2,1,0:T(2,128)(2,1)S(1)}, u32[]{:S(2)}, u32[]{:S(2)}) %all-to-all-start) | async-done | bytes 1048608 | tf_op jit(solution)/shard_map/all_to_all | solution.py:41
  95.4 3.5 %reshape.303 = bf16[128,2,4,16,32]{4,3,2,1,0:T(8,128)(2,1)} reshape(bf16[128,2,2048]{2,1,0:T(2,128)(2,1)S(1)} %all-to-all-done) | data formatting | bytes 2097152
  98.9 5.3 %copy.111 = bf16[8,2,16,16,4,32]{5,3,2,4,1,0:T(8,128)(2,1)} copy(bf16[8,2,16,16,4,32]{5,3,4,1,0,2:T(8,128)(2,1)} %bitcast.100) | data formatting | bytes 2097152 | tf_op jit(solution)/shard_map/transpose | solution.py:30
  104.2 3.9 %copy.112 = bf16[2,8,256,4,32]{2,1,0,4,3:T(8,128)(2,1)S(1)} copy(bf16[2,8,256,4,32]{4,2,3,0,1:T(8,128)(2,1)} %bitcast.101) | data formatting | bytes 2097152 | tf_op jit(solution)/shard_map/transpose | solution.py:30
  109.6 96.2 %while.26 = (s32[]{:T(128)}, bf16[8,256,128]{1,2,0:T(8,128)(2,1)S(1)}, s32[8]{0:T(128)S(1)}, s32[1,2048]{1,0:T(1,128)S(1)}, s32[2048]{0:T(1024)S(1)}, /*index=5*...) while((s32[]{:T(128)}, bf16[8,256,128]{1,2,0:T(8,128)(2,1)S(1)}, ...), condition=%wide.region_1.2_spmd, body=%wide.region_0.1_spmd.sunk | while | flops 295516672 | bytes 4611185 | solution.py:136
  110.9 5.1 %multiply_convert_fusion.3 = (bf16[128,2048]{1,0:T(8,128)(2,1)S(1)}, bf16[128,2048]{1,0:T(8,128)(2,1)S(1)}) fusion(s32[2048]{0:T(1024)S(1)} %get-tuple-element.458, s32[128]{0:T(128)S(1)} %get-tuple-element.459, s32[2048]{0:T(1024)S(1)} %get-tuple-element.460, s32[128]{0:T(128)S(1)} %get-tuple-element.461), kind=kLoop, calls=%fused_computation.56.clone.2 | loop fusion | flops 9175040 | bytes 1065984 | tf_op jit(solution)/shard_map/while/body/eval_jaxpr/convert_element_type | solution.py:101
  116.0 4.8 %fusion.126 = bf16[128,2048]{1,0:T(8,128)(2,1)S(1)} fusion(s32[2048]{0:T(1024)S(1)} %get-tuple-element.458, s32[128]{0:T(128)S(1)} %get-tuple-element.459, s32[2048]{0:T(1024)S(1)} %get-tuple-element.460, s32[128]{0:T(128)S(1)} %get-tuple-element.461), kind=kLoop, calls=%fused_computation.75.clone.1 | loop fusion | flops 9437184 | bytes 541696 | tf_op jit(solution)/shard_map/while/body/eval_jaxpr/neg | solution.py:102
  120.8 0.7 fusion.127
  123.0 5.1 %multiply_convert_fusion.3 = (bf16[128,2048]{1,0:T(8,128)(2,1)S(1)}, bf16[128,2048]{1,0:T(8,128)(2,1)S(1)}) fusion(s32[2048]{0:T(1024)S(1)} %get-tuple-element.458, s32[128]{0:T(128)S(1)} %get-tuple-element.459, s32[2048]{0:T(1024)S(1)} %get-tuple-element.460, s32[128]{0:T(128)S(1)} %get-tuple-element.461), kind=kLoop, calls=%fused_computation.56.clone.2 | loop fusion | flops 9175040 | bytes 1065984 | tf_op jit(solution)/shard_map/while/body/eval_jaxpr/convert_element_type | solution.py:101
  128.1 4.8 %fusion.126 = bf16[128,2048]{1,0:T(8,128)(2,1)S(1)} fusion(s32[2048]{0:T(1024)S(1)} %get-tuple-element.458, s32[128]{0:T(128)S(1)} %get-tuple-element.459, s32[2048]{0:T(1024)S(1)} %get-tuple-element.460, s32[128]{0:T(128)S(1)} %get-tuple-element.461), kind=kLoop, calls=%fused_computation.75.clone.1 | loop fusion | flops 9437184 | bytes 541696 | tf_op jit(solution)/shard_map/while/body/eval_jaxpr/neg | solution.py:102
  135.0 5.1 %multiply_convert_fusion.3 = (bf16[128,2048]{1,0:T(8,128)(2,1)S(1)}, bf16[128,2048]{1,0:T(8,128)(2,1)S(1)}) fusion(s32[2048]{0:T(1024)S(1)} %get-tuple-element.458, s32[128]{0:T(128)S(1)} %get-tuple-element.459, s32[2048]{0:T(1024)S(1)} %get-tuple-element.460, s32[128]{0:T(128)S(1)} %get-tuple-element.461), kind=kLoop, calls=%fused_computation.56.clone.2 | loop fusion | flops 9175040 | bytes 1065984 | tf_op jit(solution)/shard_map/while/body/eval_jaxpr/convert_element_type | solution.py:101
  140.1 4.8 %fusion.126 = bf16[128,2048]{1,0:T(8,128)(2,1)S(1)} fusion(s32[2048]{0:T(1024)S(1)} %get-tuple-element.458, s32[128]{0:T(128)S(1)} %get-tuple-element.459, s32[2048]{0:T(1024)S(1)} %get-tuple-element.460, s32[128]{0:T(128)S(1)} %get-tuple-element.461), kind=kLoop, calls=%fused_computation.75.clone.1 | loop fusion | flops 9437184 | bytes 541696 | tf_op jit(solution)/shard_map/while/body/eval_jaxpr/neg | solution.py:102
  144.9 0.7 fusion.127
  147.0 5.1 %multiply_convert_fusion.3 = (bf16[128,2048]{1,0:T(8,128)(2,1)S(1)}, bf16[128,2048]{1,0:T(8,128)(2,1)S(1)}) fusion(s32[2048]{0:T(1024)S(1)} %get-tuple-element.458, s32[128]{0:T(128)S(1)} %get-tuple-element.459, s32[2048]{0:T(1024)S(1)} %get-tuple-element.460, s32[128]{0:T(128)S(1)} %get-tuple-element.461), kind=kLoop, calls=%fused_computation.56.clone.2 | loop fusion | flops 9175040 | bytes 1065984 | tf_op jit(solution)/shard_map/while/body/eval_jaxpr/convert_element_type | solution.py:101
  152.1 4.8 %fusion.126 = bf16[128,2048]{1,0:T(8,128)(2,1)S(1)} fusion(s32[2048]{0:T(1024)S(1)} %get-tuple-element.458, s32[128]{0:T(128)S(1)} %get-tuple-element.459, s32[2048]{0:T(1024)S(1)} %get-tuple-element.460, s32[128]{0:T(128)S(1)} %get-tuple-element.461), kind=kLoop, calls=%fused_computation.75.clone.1 | loop fusion | flops 9437184 | bytes 541696 | tf_op jit(solution)/shard_map/while/body/eval_jaxpr/neg | solution.py:102
  156.9 0.7 fusion.127
  159.1 5.1 %multiply_convert_fusion.3 = (bf16[128,2048]{1,0:T(8,128)(2,1)S(1)}, bf16[128,2048]{1,0:T(8,128)(2,1)S(1)}) fusion(s32[2048]{0:T(1024)S(1)} %get-tuple-element.458, s32[128]{0:T(128)S(1)} %get-tuple-element.459, s32[2048]{0:T(1024)S(1)} %get-tuple-element.460, s32[128]{0:T(128)S(1)} %get-tuple-element.461), kind=kLoop, calls=%fused_computation.56.clone.2 | loop fusion | flops 9175040 | bytes 1065984 | tf_op jit(solution)/shard_map/while/body/eval_jaxpr/convert_element_type | solution.py:101
  164.1 4.8 %fusion.126 = bf16[128,2048]{1,0:T(8,128)(2,1)S(1)} fusion(s32[2048]{0:T(1024)S(1)} %get-tuple-element.458, s32[128]{0:T(128)S(1)} %get-tuple-element.459, s32[2048]{0:T(1024)S(1)} %get-tuple-element.460, s32[128]{0:T(128)S(1)} %get-tuple-element.461), kind=kLoop, calls=%fused_computation.75.clone.1 | loop fusion | flops 9437184 | bytes 541696 | tf_op jit(solution)/shard_map/while/body/eval_jaxpr/neg | solution.py:102
  168.9 0.7 fusion.127
  171.1 5.1 %multiply_convert_fusion.3 = (bf16[128,2048]{1,0:T(8,128)(2,1)S(1)}, bf16[128,2048]{1,0:T(8,128)(2,1)S(1)}) fusion(s32[2048]{0:T(1024)S(1)} %get-tuple-element.458, s32[128]{0:T(128)S(1)} %get-tuple-element.459, s32[2048]{0:T(1024)S(1)} %get-tuple-element.460, s32[128]{0:T(128)S(1)} %get-tuple-element.461), kind=kLoop, calls=%fused_computation.56.clone.2 | loop fusion | flops 9175040 | bytes 1065984 | tf_op jit(solution)/shard_map/while/body/eval_jaxpr/convert_element_type | solution.py:101
  176.2 4.8 %fusion.126 = bf16[128,2048]{1,0:T(8,128)(2,1)S(1)} fusion(s32[2048]{0:T(1024)S(1)} %get-tuple-element.458, s32[128]{0:T(128)S(1)} %get-tuple-element.459, s32[2048]{0:T(1024)S(1)} %get-tuple-element.460, s32[128]{0:T(128)S(1)} %get-tuple-element.461), kind=kLoop, calls=%fused_computation.75.clone.1 | loop fusion | flops 9437184 | bytes 541696 | tf_op jit(solution)/shard_map/while/body/eval_jaxpr/neg | solution.py:102
  180.9 0.7 fusion.127
  183.1 5.1 %multiply_convert_fusion.3 = (bf16[128,2048]{1,0:T(8,128)(2,1)S(1)}, bf16[128,2048]{1,0:T(8,128)(2,1)S(1)}) fusion(s32[2048]{0:T(1024)S(1)} %get-tuple-element.458, s32[128]{0:T(128)S(1)} %get-tuple-element.459, s32[2048]{0:T(1024)S(1)} %get-tuple-element.460, s32[128]{0:T(128)S(1)} %get-tuple-element.461), kind=kLoop, calls=%fused_computation.56.clone.2 | loop fusion | flops 9175040 | bytes 1065984 | tf_op jit(solution)/shard_map/while/body/eval_jaxpr/convert_element_type | solution.py:101
  188.2 4.8 %fusion.126 = bf16[128,2048]{1,0:T(8,128)(2,1)S(1)} fusion(s32[2048]{0:T(1024)S(1)} %get-tuple-element.458, s32[128]{0:T(128)S(1)} %get-tuple-element.459, s32[2048]{0:T(1024)S(1)} %get-tuple-element.460, s32[128]{0:T(128)S(1)} %get-tuple-element.461), kind=kLoop, calls=%fused_computation.75.clone.1 | loop fusion | flops 9437184 | bytes 541696 | tf_op jit(solution)/shard_map/while/body/eval_jaxpr/neg | solution.py:102
  195.1 5.1 %multiply_convert_fusion.3 = (bf16[128,2048]{1,0:T(8,128)(2,1)S(1)}, bf16[128,2048]{1,0:T(8,128)(2,1)S(1)}) fusion(s32[2048]{0:T(1024)S(1)} %get-tuple-element.458, s32[128]{0:T(128)S(1)} %get-tuple-element.459, s32[2048]{0:T(1024)S(1)} %get-tuple-element.460, s32[128]{0:T(128)S(1)} %get-tuple-element.461), kind=kLoop, calls=%fused_computation.56.clone.2 | loop fusion | flops 9175040 | bytes 1065984 | tf_op jit(solution)/shard_map/while/body/eval_jaxpr/convert_element_type | solution.py:101
  200.2 4.8 %fusion.126 = bf16[128,2048]{1,0:T(8,128)(2,1)S(1)} fusion(s32[2048]{0:T(1024)S(1)} %get-tuple-element.458, s32[128]{0:T(128)S(1)} %get-tuple-element.459, s32[2048]{0:T(1024)S(1)} %get-tuple-element.460, s32[128]{0:T(128)S(1)} %get-tuple-element.461), kind=kLoop, calls=%fused_computation.75.clone.1 | loop fusion | flops 9437184 | bytes 541696 | tf_op jit(solution)/shard_map/while/body/eval_jaxpr/neg | solution.py:102
  205.0 0.7 fusion.127
  206.6 3.8 %all_to_all.29 = bf16[4,2,2,128,4,32]{3,2,5,4,0,1:T(2,128)(2,1)S(1)} all-to-all(bf16[4,2,2,128,4,32]{3,2,5,4,0,1:T(2,128)(2,1)S(1)} %copy.115), channel_id=1, replica_groups=mesh['channel'=16,'tm'=4,'beam_0'=4,'beam_1'=2] {'beam_1'}, dimensions={1} | all-to-all | bytes 1048576 | tf_op jit(solution)/shard_map/all_to_all | solution.py:50
  210.3 1.2 copy.116
  211.6 4.2 %all-to-all-start.2 = ((bf16[4,2,2,128,4,32]{3,2,5,4,1,0:T(2,128)(2,1)}), bf16[4,2,2,128,4,32]{3,2,5,4,1,0:T(2,128)(2,1)S(1)}, u32[]{:S(2)}, u32[]{:S(2)}) async-start(bf16[4,2,2,128,4,32]{3,2,5,4,1,0:T(2,128)(2,1)} %copy.116), calls=%async_computation.2 | async-start | bytes 1048576 | tf_op jit(solution)/shard_map/all_to_all | solution.py:50
  218.1 11.7 %all-to-all-done.2 = bf16[4,2,2,128,4,32]{3,2,5,4,1,0:T(2,128)(2,1)S(1)} async-done(((bf16[4,2,2,128,4,32]{3,2,5,4,1,0:T(2,128)(2,1)}), bf16[4,2,2,128,4,32]{3,2,5,4,1,0:T(2,128)(2,1)S(1)}, u32[]{:S(2)}, u32[]{:S(2)}) %all-to-all-start.2) | async-done | bytes 524320 | tf_op jit(solution)/shard_map/all_to_all | solution.py:50
  230.0 3.2 collective-permute-start
  233.8 3.0 collective-permute-done
  236.8 1.8 multiply_add_fusion
  240.0 1.0 fusion.58
  241.3 0.9 convert_element_type.152
  242.2 5.1 %all-to-all-start.3 = ((bf16[128,4,256]{2,1,0:T(4,128)(2,1)}), bf16[128,4,256]{2,1,0:T(4,128)(2,1)S(1)}, u32[]{:S(2)}, u32[]{:S(2)}) async-start(bf16[128,4,256]{2,1,0:T(4,128)(2,1)} %convert_element_type.152), calls=%async_computation.3 | async-start | bytes 524288 | tf_op jit(solution)/shard_map/all_to_all | solution.py:162
  247.3 5.5 %all-to-all-done.3 = bf16[128,4,256]{2,1,0:T(4,128)(2,1)S(1)} async-done(((bf16[128,4,256]{2,1,0:T(4,128)(2,1)}), bf16[128,4,256]{2,1,0:T(4,128)(2,1)S(1)}, u32[]{:S(2)}, u32[]{:S(2)}) %all-to-all-start.3) | async-done | bytes 262176 | tf_op jit(solution)/shard_map/all_to_all | solution.py:162
  253.7 1.5 subtract_bitcast_fusion
  255.2 2.8 copy.126
  258.0 3.2 fusion.111
  261.2 1.2 copy.127
  262.4 29.8 %while.27 = (s32[]{:T(128)}, f32[4,16,32,256]{3,2,1,0:T(8,128)}, f32[2,64,32,64]{3,2,1,0:T(8,128)S(1)}, s32[4]{0:T(128)S(1)}, s32[64,128]{1,0:T(8,128)S(1)}, /*index=5*/s32[]{:T(128)}, s32[]{:T(128)}, s32[]{:T(128)}) while((s32[]{:T(128)}, f32[4,16,32,256]{3,2,1,0:T(8,128)}, f32[2,64,32,64]{3,2,1,0:T(8,128)S(1)}, s32[4]{0:T(128)S(1)}, ...), condition=%wide.region_5.6_spmd, body=%wide.region_4.5_spmd.sunk | while | flops 204931088 | bytes 6587147 | solution.py:200
  265.8 2.1 fusion.130
  268.0 1.9 fusion.132
  273.3 2.1 fusion.130
  275.4 1.9 fusion.132
  280.7 2.1 fusion.130
  282.8 1.9 fusion.132
  288.2 2.1 fusion.130
  290.3 1.9 fusion.132
  292.2 2.5 reshape.289
  294.7 2.5 fusion.55
  298.0 1.5 reshape.304
  299.5 4.3 %all-to-all-start.4 = ((bf16[16,2,8192]{2,1,0:T(2,128)(2,1)}), bf16[16,2,8192]{2,1,0:T(2,128)(2,1)S(1)}, u32[]{:S(2)}, u32[]{:S(2)}) async-start(bf16[16,2,8192]{2,1,0:T(2,128)(2,1)} %reshape.304), calls=%async_computation.4 | async-start | bytes 1048576 | tf_op jit(solution)/shard_map/all_to_all | solution.py:76
  304.2 1.2 reshape.300
  305.4 25.7 %all-to-all-done.4 = bf16[16,2,8192]{2,1,0:T(2,128)(2,1)S(1)} async-done(((bf16[16,2,8192]{2,1,0:T(2,128)(2,1)}), bf16[16,2,8192]{2,1,0:T(2,128)(2,1)S(1)}, u32[]{:S(2)}, u32[]{:S(2)}) %all-to-all-start.4) | async-done | bytes 524320 | tf_op jit(solution)/shard_map/all_to_all | solution.py:76
  331.7 0.9 convert_reduce_fusion
  (125 shorter events, 27.3 us)
Async XLA Ops:
  18.9 20.5 %copy-start.2 = (s32[2048]{0:T(1024)S(1)}, s32[2048]{0:T(1024)}, u32[]{:S(2)}) copy-start(s32[2048]{0:T(1024)} %param.8) | copy-start | bytes 24580
  18.9 76.5 %all-to-all-start = ((bf16[128,2,2048]{2,1,0:T(2,128)(2,1)}), bf16[128,2,2048]{2,1,0:T(2,128)(2,1)S(1)}, u32[]{:S(2)}, u32[]{:S(2)}) async-start(bf16[128,2,2048]{2,1,0:T(2,128)(2,1)} %reshape.302), calls=%async_computation | async-start | bytes 2097152 | tf_op jit(solution)/shard_map/all_to_all | solution.py:41
  108.6 1.0 copy-start.1
  211.6 18.3 %all-to-all-start.2 = ((bf16[4,2,2,128,4,32]{3,2,5,4,1,0:T(2,128)(2,1)}), bf16[4,2,2,128,4,32]{3,2,5,4,1,0:T(2,128)(2,1)S(1)}, u32[]{:S(2)}, u32[]{:S(2)}) async-start(bf16[4,2,2,128,4,32]{3,2,5,4,1,0:T(2,128)(2,1)} %copy.116), calls=%async_computation.2 | async-start | bytes 1048576 | tf_op jit(solution)/shard_map/all_to_all | solution.py:50
  230.0 6.8 %collective-permute-start = (bf16[2,128,4,112]{1,3,2,0:T(8,128)(2,1)S(1)}, bf16[2,128,4,112]{1,3,2,0:T(8,128)(2,1)S(1)}, u32[]{:S(2)}, u32[]{:S(2)}) collective-permute-start(bf16[2,128,4,112]{1,3,2,0:T(8,128)(2,1)S(1)} %slice.102), channel_id=1, source_target_pairs={{0,8},{8,16},{16,24},{1,9},{9,17},{17,25},{2,10},{10,18},{18,26},{... | collective-permute-start | bytes 688136 | tf_op jit(solution)/shard_map/ppermute | solution.py:63
  242.2 10.6 %all-to-all-start.3 = ((bf16[128,4,256]{2,1,0:T(4,128)(2,1)}), bf16[128,4,256]{2,1,0:T(4,128)(2,1)S(1)}, u32[]{:S(2)}, u32[]{:S(2)}) async-start(bf16[128,4,256]{2,1,0:T(4,128)(2,1)} %convert_element_type.152), calls=%async_computation.3 | async-start | bytes 524288 | tf_op jit(solution)/shard_map/all_to_all | solution.py:162
  261.1 1.2 copy-start
  299.5 31.5 %all-to-all-start.4 = ((bf16[16,2,8192]{2,1,0:T(2,128)(2,1)}), bf16[16,2,8192]{2,1,0:T(2,128)(2,1)S(1)}, u32[]{:S(2)}, u32[]{:S(2)}) async-start(bf16[16,2,8192]{2,1,0:T(2,128)(2,1)} %reshape.304), calls=%async_computation.4 | async-start | bytes 1048576 | tf_op jit(solution)/shard_map/all_to_all | solution.py:76
where the time goes:
time: 336 us; the launch traced here: 333 us
  waiting for transfers between devices  102 us (30%)
  other arithmetic  101 us (30%)
  local copies, waits for them, and re-layouts  58.2 us (17%)
  starting transfers between devices  37.4 us (11%)
  matrix products  20 us (6%)
  loops' own time  8.41 us (3%)
  blocking collectives  3.79 us (1%)
    all_to_all x1, waiting for transfers between devices, exchange_both(): parts = lax.all_to_all(parts, axis, split_axis=0, concat_axis=0, tiled=True)  55.9 us
    convert_element_type x8, other arithmetic, steering(): w_imag = (-jnp.sin(angles) * norm_scale).astype(jnp.bfloat16)  40.6 us
    neg x8, other arithmetic, steering(): top_half = jnp.concatenate([w_real, -w_imag], axis=1)  38.1 us
    all_to_all x1, waiting for transfers between devices, sent_and_summed(): lax.all_to_all(parts, axis, split_axis=0, concat_axis=0, tiled=True)  25.7 us
    all_to_all x1, starting transfers between devices, exchange_both(): parts = lax.all_to_all(parts, axis, split_axis=0, concat_axis=0, tiled=True)  20.5 us
    unnamed x12, local copies, waits for them, and re-layouts  14.8 us
    all_to_all x1, waiting for transfers between devices, moved_by_axis(): out = lax.all_to_all(out, axes[k], k, k, tiled=True)  11.7 us
    transpose x2, local copies, waits for them, and re-layouts, laid_out(): parts = jnp.moveaxis(parts, 0, dim)  9.17 us
  transfers between devices with their start and end apart: 5, of which 5 were waited for; matrix products, arithmetic and copies ran while one was open for 1% of the time, Pallas kernels for 0%

commit v1 on v0

v1 whole, which is shorter than its diff:
```python
import functools
import math

import jax
import jax.numpy as jnp
import numpy as np
from jax import lax
from jax.experimental import pallas as pl
from jax.experimental.pallas import tpu as pltpu
from jax.sharding import Mesh
from jax.sharding import PartitionSpec as P

F32 = jnp.float32
BF16 = jnp.bfloat16
FEEDS = 2048
TAPS = 8
UPCH = 16
FRAMES = 64
FINE = 1024


def cos_turns(steps, period):
    left = (steps & (period - 1)) - period // 2
    u = jnp.abs(left).astype(F32) * (4.0 / period) - 1.0
    u2 = u * u
    p = -3.598843235e-06
    for c in (1.604411848e-04, -4.681754135e-03, 7.969262625e-02, -6.459640975e-01, 1.570796327e00):
        p = p * u2 + c
    return p * u


def split(value):
    high = value.astype(BF16)
    return high, (value - high.astype(F32)).astype(BF16)


def mm(a, b):
    return jnp.dot(a, b, preferred_element_type=F32)


def table_split(table):
    table = jnp.asarray(table.astype(np.float32))
    high = table.astype(BF16)
    return high, (table - high.astype(F32)).astype(BF16)


def north_table():
    n = np.arange(256)
    angle = 2 * np.pi * (n[:, None] * n[None, :] % 256) / 256
    return np.concatenate([np.cos(angle), np.sin(angle)], axis=1) / math.sqrt(FEEDS)


def filter_table():
    length = TAPS * UPCH
    j = np.arange(length)
    h = np.sinc((j - (length - 1) / 2) / UPCH) * (0.5 - 0.5 * np.cos(2 * np.pi * (j + 0.5) / length))
    h = h / np.sqrt(np.sum(h * h))
    s = np.arange(256)
    out = np.arange(128)
    tap = (s[:, None] // 16 - 8) - out[None, :] // 16 + 7
    m = s % 16
    used = (tap >= 0) & (tap < 8)
    weight = np.where(used, h[np.clip(tap, 0, 7) * 16 + m[:, None]], 0.0)
    angle = 2 * np.pi * (m[:, None] * (out % 16)[None, :] % 16) / 16
    c = (weight * np.cos(angle)).reshape(2, 128, 128)
    d = (weight * np.sin(angle)).reshape(2, 128, 128)
    real_in = np.concatenate([c, -d], axis=2)
    imag_in = np.concatenate([d, c], axis=2)
    return np.stack([real_in, imag_in], axis=1).reshape(512, 256)


def relayout(v_ref, s_ref):
    for g in range(8):
        for h in range(2):
            x = v_ref[:, :, g * 8 : g * 8 + 8, h * 128 : h * 128 + 128]
            x = x.astype(F32).reshape(32, 8, 128)
            y = jnp.swapaxes(x, 0, 1).astype(BF16)
            for c in range(8):
                s_ref[(g * 8 + c) * 2 + h] = y[c]


def fill_places(pos_ref, oh_ref):
    pos = pos_ref[...]

    def body(i, carry):
        row = lax.broadcasted_iota(jnp.int32, (128, FEEDS), 0) + i * 128
        hit = jnp.where(row == pos, 1.0, 0.0).astype(BF16)
        oh_ref[pl.ds(pl.multiple_of(i * 128, 128), 128), :] = hit
        return carry

    lax.fori_loop(0, 8, body, 0)


def beamform(oh_ref, r1_ref, a_hi_ref, a_lo_ref, b_ref):
    xr = r1_ref[:, 0:16, :].reshape(FEEDS, 128)
    xi = r1_ref[:, 16:32, :].reshape(FEEDS, 128)
    x = jnp.concatenate([xr, xi], axis=1)
    re, im = [], []
    for c in range(4):
        g = mm(oh_ref[c * 256 : c * 256 + 256, :], x)
        re.append(g[:, :128])
        im.append(g[:, 128:])
    a_hi, a_lo = a_hi_ref[...], a_lo_ref[...]
    er, ei = re[0] + re[2], im[0] + im[2]
    fr, fi = re[1] + re[3], im[1] + im[3]
    dr, di = re[0] - re[2], im[0] - im[2]
    gr, gi = re[1] - re[3], im[1] - im[3]
    parts = [(er + fr, ei + fi), (dr + gi, di - gr), (er - fr, ei - fi), (dr - gi, di + gr)]
    for be in range(4):
        hr, hi = parts[be]
        top = jnp.concatenate([hr, hi], axis=1)
        low = jnp.concatenate([hi, -hr], axis=1)
        b_hi, b_lo = split(jnp.concatenate([top, low], axis=0))
        res = (mm(a_hi, b_hi) + (mm(a_hi, b_lo) + mm(a_lo, b_hi))).astype(BF16)
        b_ref[be * 8 : be * 8 + 8, 0] = res[:, :128].reshape(8, 32, 128)
        b_ref[be * 8 : be * 8 + 8, 1] = res[:, 128:].reshape(8, 32, 128)


def fill_spectrum(f_ref):
    def body(i, carry):
        row = lax.broadcasted_iota(jnp.int32, (128, 1024), 0) + i * 128
        lane = lax.broadcasted_iota(jnp.int32, (128, 1024), 1)
        w = (row >> 5) + 1
        steps = w * (lane >> 4) + ((row >> 4) & 1) * 16
        value = jnp.where((row & 15) == (lane & 15), cos_turns(steps, 64), 0.0)
        f_ref[pl.ds(pl.multiple_of(i * 128, 128), 128), :] = value.astype(BF16)
        return carry

    lax.fori_loop(0, 8, body, 0)


def fill_trials(delay_ref, tab_ref):
    dt = jnp.transpose(delay_ref[...].astype(F32)).astype(jnp.int32)
    dd = jnp.concatenate([dt, dt], axis=1)
    rows = []
    for rb in range(32):
        d = ((rb // 2) % 4) * 4 + rb // 8
        rows.append(dd[d * 8 : d * 8 + 8, :])
    step = jnp.concatenate(rows, axis=0)
    row = lax.broadcasted_iota(jnp.int32, (256, 128), 0)
    lane = lax.broadcasted_iota(jnp.int32, (256, 128), 1)
    start = 64 + 16 * (((row >> 3) & 1) - (lane >> 6))

    def body(q, phase):
        for k in range(4):
            phase = phase + step
            tab_ref[q, :, k * 128 : k * 128 + 128] = cos_turns(phase, 64).astype(BF16)
        return phase

    lax.fori_loop(0, 8, body, start)


def fill_inverse(m_ref):
    for w4 in range(4):
        row = lax.broadcasted_iota(jnp.int32, (128, 512), 0)
        lane = lax.broadcasted_iota(jnp.int32, (128, 512), 1)
        w = (row >> 4) * 4 + w4 + 1
        steps = w * (lane & 63) + ((row >> 3) & 1) * 16
        value = jnp.where((row & 7) == (lane >> 6), cos_turns(steps, 64), 0.0)
        scale = jnp.where(w == FRAMES // 2, 1.0, 2.0) * (1.0 / (FRAMES * math.sqrt(FINE)))
        m_ref[w4] = value * scale


def power(block, c_hi_ref, c_lo_ref, out_ref, cc_ref):
    c_hi, c_lo = c_hi_ref[...], c_lo_ref[...]
    zero = jnp.zeros((32, 128), BF16)
    for j in range(4):
        cur = [jnp.concatenate([block(j, t, r) for t in range(8)], axis=0) for r in range(2)]
        old = [jnp.concatenate([zero, cur[r][:224]], axis=0) for r in range(2)]
        left = jnp.concatenate(old + cur, axis=1)
        y = mm(left, c_hi) + mm(left, c_lo)
        p = y[:, :128] * y[:, :128] + y[:, 128:] * y[:, 128:]
        total = p[0:32]
        for t in range(1, 8):
            total = total + p[t * 32 : t * 32 + 32]
        for shift in (16, 32, 64):
            total = total + pltpu.roll(total, shift, 1)
        mean = total * (1.0 / FRAMES)
        for t in range(8):
            pt = p[t * 32 : t * 32 + 32]
            out_ref[pl.ds(t * 4 + j, 32, stride=32), :] = pt
            cc_ref[j * 32 : j * 32 + 32, t * 128 : t * 128 + 128] = (pt - mean).astype(BF16)


def dedisperse(f_ref, cc_ref, tab_ref, z_ref):
    cc = cc_ref[...]
    group = lax.broadcasted_iota(jnp.int32, (16, 128), 1) >> 5
    for q in range(8):
        s = lax.dot_general(
            f_ref[q * 128 : q * 128 + 128, :], cc, (((1,), (1,)), ((), ())), preferred_element_type=F32
        )
        turned = [s] + [pltpu.roll(s, 32 * k, 1) for k in range(1, 4)]
        rows = []
        for w4 in range(4):
            for r in range(2):
                for j in range(4):
                    at = (w4 * 2 + r) * 16
                    part = turned[(w4 - j) % 4][at : at + 16]
                    rows.append(jnp.where(group == w4, part, 0.0).astype(BF16))
        right = jnp.concatenate(rows, axis=0)
        z = mm(tab_ref[q], right).astype(BF16)
        z_ref[:, :, q * 128 : q * 128 + 128] = z.reshape(4, 64, 128)


def series(zs, m_ref, out_ref):
    v = jnp.concatenate([zs[:, q * 128 : q * 128 + 128] for q in range(8)], axis=0)
    vt = jnp.transpose(v)
    res = jnp.zeros((32, 512), F32)
    for w4 in range(4):
        res = res + jnp.dot(
            vt[w4 * 32 : w4 * 32 + 32], m_ref[w4], precision=lax.Precision.HIGHEST, preferred_element_type=F32
        )
    for d in range(8):
        out_ref[pl.ds(d, 32, stride=8), :] = res[:, d * 64 : d * 64 + 64]


def call(kernel, out, scratch=(), **kw):
    outs = out if isinstance(out, (list, tuple)) else [out]
    spec = pl.BlockSpec(memory_space=pltpu.VMEM)

    def run(*args):
        return pl.pallas_call(
            kernel,
            out_shape=out,
            in_specs=[spec] * len(args),
            out_specs=spec if not isinstance(out, (list, tuple)) else [spec] * len(outs),
            scratch_shapes=list(scratch),
            compiler_params=pltpu.CompilerParams(vmem_limit_bytes=60 << 20),
            **kw,
        )(*args)

    return run


def k_relayout(v_ref, s_ref):
    relayout(v_ref, s_ref)


def k_beam(pos_ref, r1_ref, ah_ref, al_ref, b_ref, oh_ref):
    fill_places(pos_ref, oh_ref)
    beamform(oh_ref, r1_ref, ah_ref, al_ref, b_ref)


def k_power(r2_ref, ch_ref, cl_ref, delay_ref, i_ref, z_ref, cc_ref, f_ref, tab_ref):
    fill_spectrum(f_ref)
    fill_trials(delay_ref, tab_ref)

    def block(j, t, r):
        return r2_ref[j, t % 2, t // 2, r]

    power(block, ch_ref, cl_ref, i_ref, cc_ref)
    dedisperse(f_ref, cc_ref, tab_ref, z_ref)


def k_series(z_ref, o_ref, m_ref):
    fill_inverse(m_ref)
    zs = z_ref[0].astype(F32)
    for k in range(1, 4):
        zs = zs + z_ref[k].astype(F32)
    series(zs, m_ref, o_ref)


def S(shape, dtype):
    return jax.ShapeDtypeStruct(shape, dtype)


run_relayout = call(k_relayout, S((128, 32, 128), BF16))
run_beam = call(k_beam, S((32, 2, 32, 128), BF16), [pltpu.VMEM((1024, FEEDS), BF16)])
run_power = call(
    k_power,
    [S((1024, 128), F32), S((4, 64, 1024), BF16)],
    [pltpu.VMEM((128, 1024), BF16), pltpu.VMEM((1024, 1024), BF16), pltpu.VMEM((8, 256, 512), BF16)],
)
run_series = call(k_series, S((256, 64), F32), [pltpu.VMEM((4, 128, 512), F32)])


def per_device(voltages, positions, delays):
    a_hi, a_lo = table_split(north_table())
    c_hi, c_lo = table_split(filter_table())
    s1 = run_relayout(voltages)
    r1 = lax.all_to_all(s1, ("z_hi", "x", "z_lo", "core"), 0, 0, tiled=True)
    pos = positions.reshape(8, 16, 16).swapaxes(0, 1).reshape(1, FEEDS)
    b = run_beam(pos, r1, a_hi, a_lo)
    r2 = lax.all_to_all(b, ("z_lo", "core", "tm"), 0, 0, tiled=True)
    i, z = run_power(r2.reshape(4, 2, 4, 2, 32, 128), c_hi, c_lo, delays.T)
    z = lax.all_to_all(z, "x", 0, 0, tiled=True)
    z = z.astype(F32).sum(axis=0).astype(BF16).reshape(4, 16, 1024)
    z = lax.all_to_all(z, "z_hi", 0, 0, tiled=True)
    d = run_series(z)
    i = i.reshape(32, 8, 4, 128).swapaxes(1, 2).reshape(32, 4, 1024)
    return i, d.reshape(32, 8, 64)


def solution(mesh):
    finer = Mesh(mesh.devices.reshape(4, 4, 4, 4, 2), ("z_hi", "x", "tm", "z_lo", "core"))
    beam, channel = ("z_lo", "core"), ("z_hi", "x")
    return jax.shard_map(
        per_device,
        mesh=finer,
        in_specs=(P(None, beam + channel, None, "tm"), P(), P(None, channel)),
        out_specs=(P(beam + ("tm",), channel, None), P(beam + ("tm",), channel, None)),
        check_vma=False,
    )
```

time: 336 us -> 155 us (0.46)
  other arithmetic: 101 us -> 0.08 us
  local copies, waits for them, and re-layouts: 58.2 us -> 1.77 us
  blocking collectives: 3.79 us -> 52.9 us
  waiting for transfers between devices: 102 us -> 55.1 us
  Pallas kernels: 0 us -> 22.4 us
  matrix products: 20 us -> 0 us
  starting transfers between devices: 37.4 us -> 20.5 us
  loops' own time: 8.41 us -> 0 us
    all_to_all x1 -> x3, blocking collectives: 3.79 us -> 52.9 us  [the longest x1 23.8 us: per_device(): r2 = lax.all_to_all(b, ('z_lo', 'core', 'tm'), 0, 0, tiled=True)]
    neg x14 -> x0, other arithmetic: 46.9 us -> none  [the longest x8 38.1 us: steering(): top_half = jnp.concatenate([w_real, -w_imag], axis=1)]
    all_to_all x4 -> x1, waiting for transfers between devices: 98.8 us -> 55.1 us  [per_device(): r1 = lax.all_to_all(s1, ('z_hi', 'x', 'z_lo', 'core'), 0, 0, tiled=True)]
    convert_element_type x10 -> x0, other arithmetic: 40.7 us -> none  [the longest x8 40.6 us: steering(): w_imag = (-jnp.sin(angles) * norm_scale).astype(jnp.bfloat16)]
    pallas_call x0 -> x4, Pallas kernels: none -> 22.4 us  [run(): pl.pallas_call(kernel, out_shape=out, in_specs=[spec] * len(args), out_sp...]
    dot_general x15 -> x0, matrix products: 20 us -> none  [the longest x4 7.64 us: dedisperse(): return jnp.einsum('vbk,vkd->vbd', left_side, table, precision=HIGHEST)]
    unnamed x12 -> x4, local copies, waits for them, and re-layouts: 14.8 us -> 0.98 us
    all_to_all x4 -> x1, starting transfers between devices: 34.1 us -> 20.5 us  [per_device(): r1 = lax.all_to_all(s1, ('z_hi', 'x', 'z_lo', 'core'), 0, 0, tiled=True)]
  transfers between devices with their start and end apart: 5 -> 1, of which waited for: 5 -> 1; matrix products, arithmetic and copies ran while one was open for 1% -> 1% of each run, Pallas kernels for 0% -> 0%
where the time goes in v1:
time: 155 us; the launch traced here: 153 us
  waiting for transfers between devices  55.1 us (36%)
  blocking collectives  52.9 us (34%)
  Pallas kernels  22.4 us (14%)
  starting transfers between devices  20.5 us (13%)
  local copies, waits for them, and re-layouts  1.77 us (1%)
    all_to_all x1, waiting for transfers between devices, per_device(): r1 = lax.all_to_all(s1, ('z_hi', 'x', 'z_lo', 'core'), 0, 0, tiled=True)  55.1 us
    all_to_all x1, blocking collectives, per_device(): r2 = lax.all_to_all(b, ('z_lo', 'core', 'tm'), 0, 0, tiled=True)  23.8 us
    pallas_call x4, Pallas kernels, run(): pl.pallas_call(kernel, out_shape=out, in_specs=[spec] * len(args), out_sp...  22.4 us
    all_to_all x1, starting transfers between devices, per_device(): r1 = lax.all_to_all(s1, ('z_hi', 'x', 'z_lo', 'core'), 0, 0, tiled=True)  20.5 us
    all_to_all x1, blocking collectives, per_device(): z = lax.all_to_all(z, 'z_hi', 0, 0, tiled=True)  16.4 us
    all_to_all x1, blocking collectives, per_device(): z = lax.all_to_all(z, 'x', 0, 0, tiled=True)  12.6 us
  transfers between devices with their start and end apart: 1, of which 1 were waited for; matrix products, arithmetic and copies ran while one was open for 1% of the time, Pallas kernels for 0%

profile of v1, /device:TPU:1, one launch (start us, length us, event | category | flops | bytes accessed | tf_op | source)
XLA Modules:
  0.0 153.4 jit_solution(9550097130294111954)
XLA Ops:
  0.6 2.7 %shard_map.68 = bf16[128,32,128]{2,1,0:T(8,128)(2,1)} custom-call(bf16[2,16,64,256]{3,2,1,0:T(8,128)(2,1)} %v_ref.1), custom_call_target="tpu_custom_call" | custom-call | tf_op jit(solution)/shard_map/pallas_call | solution.py:222
  3.3 0.0 copy-start.1
  3.3 20.5 %all-to-all-start = ((bf16[128,32,128]{2,1,0:T(8,128)(2,1)}), bf16[128,32,128]{2,1,0:T(8,128)(2,1)S(1)}, u32[]{:S(2)}, u32[]{:S(2)}) async-start(bf16[128,32,128]{2,1,0:T(8,128)(2,1)} %shard_map.68), calls=%async_computation | async-start | bytes 2097152 | tf_op jit(solution)/shard_map/all_to_all | solution.py:281
  23.9 0.0 copy-done.1
  23.9 0.1 reshape.25
  24.0 0.7 reshape.26.pos_ref
  24.7 55.1 %all-to-all-done.r1_ref = bf16[128,32,128]{2,1,0:T(8,128)(2,1)S(1)} async-done(((bf16[128,32,128]{2,1,0:T(8,128)(2,1)}), bf16[128,32,128]{2,1,0:T(8,128)(2,1)S(1)}, u32[]{:S(2)}, u32[]{:S(2)}) %all-to-all-start) | async-done | bytes 1048608 | tf_op jit(solution)/shard_map/all_to_all | solution.py:281
  79.8 0.0 copy-start
  79.8 1.0 copy-done
  80.8 5.1 %shard_map.69 = bf16[32,2,32,128]{3,2,1,0:T(8,128)(2,1)} custom-call(s32[1,2048]{1,0:T(1,128)} %reshape.26.pos_ref, bf16[128,32,128]{2,1,0:T(8,128)(2,1)} %copy-done, bf16[256,512]{1,0:T(8,128)(2,1)} %constant.10.ah_ref, bf16[256,512]{1,0:T(8,128)(2,1)} %constant.13.al_ref), custom_call_target="tpu_custom_call" | custom-call | tf_op jit(solution)/shard_map/pallas_call | solution.py:222
  85.9 23.8 %all_to_all.20 = bf16[32,2,32,128]{3,2,1,0:T(8,128)(2,1)} all-to-all(bf16[32,2,32,128]{3,2,1,0:T(8,128)(2,1)} %shard_map.69), channel_id=1, replica_groups=mesh['z_hi'=4,'x'=4,'tm'=4,'z_lo'=4,'core'=2] {'z_lo','core','tm'}, dimensions={0} | all-to-all | bytes 1048576 | tf_op jit(solution)/shard_map/all_to_all | solution.py:284
  109.8 11.4 %shard_map.70 = (f32[1024,128]{1,0:T(8,128)}, bf16[4,64,1024]{2,1,0:T(8,128)(2,1)}) custom-call(bf16[4,2,4,2,32,128]{5,4,3,2,1,0:T(8,128)(2,1)} %bitcast.10, bf16[512,256]{1,0:T(8,128)(2,1)} %constant.14.ch_ref, bf16[512,256]{1,0:T(8,128)(2,1)} %constant.17.cl_ref, s32[64,128]{1,0:T(8,128)} %bitcast.14), custom_call_target="tpu_custom_call" | custom-call | tf_op jit(solution)/shard_map/pallas_call | solution.py:222
  121.2 12.6 %all_to_all.21 = bf16[4,64,1024]{2,1,0:T(8,128)(2,1)S(1)} all-to-all(bf16[4,64,1024]{2,1,0:T(8,128)(2,1)} %get-tuple-element.5), channel_id=1, replica_groups=mesh['z_hi'=4,'x'=4,'tm'=4,'z_lo'=4,'core'=2] {'x'}, dimensions={0} | all-to-all | bytes 1048576 | tf_op jit(solution)/shard_map/all_to_all | solution.py:286
  133.8 0.1 reduce_sum.12
  133.9 16.4 %all_to_all.22.z_ref = bf16[4,16,1024]{2,1,0:T(8,128)(2,1)} all-to-all(bf16[4,16,1024]{2,1,0:T(8,128)(2,1)S(1)} %bitcast.11), channel_id=1, replica_groups=mesh['z_hi'=4,'x'=4,'tm'=4,'z_lo'=4,'core'=2] {'z_hi'}, dimensions={0} | all-to-all | bytes 262144 | tf_op jit(solution)/shard_map/all_to_all | solution.py:288
  150.3 3.1 %shard_map.71 = f32[256,64]{1,0:T(8,128)} custom-call(bf16[4,16,1024]{2,1,0:T(8,128)(2,1)} %all_to_all.22.z_ref), custom_call_target="tpu_custom_call" | custom-call | tf_op jit(solution)/shard_map/pallas_call | solution.py:222
  (1 shorter events, 0.0 us)
Async XLA Ops:
  3.3 20.5 %copy-start.1 = (s32[2048]{0:T(1024)S(1)}, s32[2048]{0:T(1024)}, u32[]{:S(2)}) copy-start(s32[2048]{0:T(1024)} %param.6) | copy-start | bytes 24580
  3.3 76.5 %all-to-all-start = ((bf16[128,32,128]{2,1,0:T(8,128)(2,1)}), bf16[128,32,128]{2,1,0:T(8,128)(2,1)S(1)}, u32[]{:S(2)}, u32[]{:S(2)}) async-start(bf16[128,32,128]{2,1,0:T(8,128)(2,1)} %shard_map.68), calls=%async_computation | async-start | bytes 2097152 | tf_op jit(solution)/shard_map/all_to_all | solution.py:281
  79.8 1.0 copy-start

commit v2 on v1

--- a/solution.py
+++ b/solution.py
@@ -1,4 +1,3 @@
-import functools
 import math
 
 import jax
@@ -7,7 +6,6 @@
 from jax import lax
 from jax.experimental import pallas as pl
 from jax.experimental.pallas import tpu as pltpu
-from jax.sharding import Mesh
 from jax.sharding import PartitionSpec as P
 
 F32 = jnp.float32
@@ -91,7 +89,7 @@
     lax.fori_loop(0, 8, body, 0)
 
 
-def beamform(oh_ref, r1_ref, a_hi_ref, a_lo_ref, b_ref):
+def grid_sums(oh_ref, r1_ref, hh_ref, hl_ref):
     xr = r1_ref[:, 0:16, :].reshape(FEEDS, 128)
     xi = r1_ref[:, 16:32, :].reshape(FEEDS, 128)
     x = jnp.concatenate([xr, xi], axis=1)
@@ -100,7 +98,6 @@
         g = mm(oh_ref[c * 256 : c * 256 + 256, :], x)
         re.append(g[:, :128])
         im.append(g[:, 128:])
-    a_hi, a_lo = a_hi_ref[...], a_lo_ref[...]
     er, ei = re[0] + re[2], im[0] + im[2]
     fr, fi = re[1] + re[3], im[1] + im[3]
     dr, di = re[0] - re[2], im[0] - im[2]
@@ -110,10 +107,14 @@
         hr, hi = parts[be]
         top = jnp.concatenate([hr, hi], axis=1)
         low = jnp.concatenate([hi, -hr], axis=1)
-        b_hi, b_lo = split(jnp.concatenate([top, low], axis=0))
-        res = (mm(a_hi, b_hi) + (mm(a_hi, b_lo) + mm(a_lo, b_hi))).astype(BF16)
-        b_ref[be * 8 : be * 8 + 8, 0] = res[:, :128].reshape(8, 32, 128)
-        b_ref[be * 8 : be * 8 + 8, 1] = res[:, 128:].reshape(8, 32, 128)
+        hh_ref[be], hl_ref[be] = split(jnp.concatenate([top, low], axis=0))
+
+
+def north_beams(be, hh_ref, hl_ref, a_hi, a_lo, b_ref):
+    b_hi, b_lo = hh_ref[be], hl_ref[be]
+    res = (mm(a_hi, b_hi) + (mm(a_hi, b_lo) + mm(a_lo, b_hi))).astype(BF16)
+    b_ref[pl.ds(be * 8, 8), 0] = res[:, :128].reshape(8, 32, 128)
+    b_ref[pl.ds(be * 8, 8), 1] = res[:, 128:].reshape(8, 32, 128)
 
 
 def fill_spectrum(f_ref):
@@ -182,28 +183,24 @@
             cc_ref[j * 32 : j * 32 + 32, t * 128 : t * 128 + 128] = (pt - mean).astype(BF16)
 
 
-def dedisperse(f_ref, cc_ref, tab_ref, z_ref):
-    cc = cc_ref[...]
+def bin_quad(q, f_ref, cc_ref, tab_ref):
     group = lax.broadcasted_iota(jnp.int32, (16, 128), 1) >> 5
-    for q in range(8):
-        s = lax.dot_general(
-            f_ref[q * 128 : q * 128 + 128, :], cc, (((1,), (1,)), ((), ())), preferred_element_type=F32
-        )
-        turned = [s] + [pltpu.roll(s, 32 * k, 1) for k in range(1, 4)]
-        rows = []
-        for w4 in range(4):
-            for r in range(2):
-                for j in range(4):
-                    at = (w4 * 2 + r) * 16
-                    part = turned[(w4 - j) % 4][at : at + 16]
-                    rows.append(jnp.where(group == w4, part, 0.0).astype(BF16))
-        right = jnp.concatenate(rows, axis=0)
-        z = mm(tab_ref[q], right).astype(BF16)
-        z_ref[:, :, q * 128 : q * 128 + 128] = z.reshape(4, 64, 128)
-
-
-def series(zs, m_ref, out_ref):
-    v = jnp.concatenate([zs[:, q * 128 : q * 128 + 128] for q in range(8)], axis=0)
+    s = lax.dot_general(
+        f_ref[q * 128 : q * 128 + 128, :], cc_ref[...], (((1,), (1,)), ((), ())), preferred_element_type=F32
+    )
+    turned = [s] + [pltpu.roll(s, 32 * k, 1) for k in range(1, 4)]
+    rows = []
+    for w4 in range(4):
+        for r in range(2):
+            for j in range(4):
+                at = (w4 * 2 + r) * 16
+                part = turned[(w4 - j) % 4][at : at + 16]
+                rows.append(jnp.where(group == w4, part, 0.0).astype(BF16))
+    right = jnp.concatenate(rows, axis=0)
+    return mm(tab_ref[q], right).astype(BF16).reshape(4, 64, 128)
+
+
+def series(v, m_ref, out_ref):
     vt = jnp.transpose(v)
     res = jnp.zeros((32, 512), F32)
     for w4 in range(4):
@@ -214,90 +211,212 @@
         out_ref[pl.ds(d, 32, stride=8), :] = res[:, d * 64 : d * 64 + 64]
 
 
-def call(kernel, out, scratch=(), **kw):
-    outs = out if isinstance(out, (list, tuple)) else [out]
-    spec = pl.BlockSpec(memory_space=pltpu.VMEM)
-
-    def run(*args):
-        return pl.pallas_call(
-            kernel,
-            out_shape=out,
-            in_specs=[spec] * len(args),
-            out_specs=spec if not isinstance(out, (list, tuple)) else [spec] * len(outs),
-            scratch_shapes=list(scratch),
-            compiler_params=pltpu.CompilerParams(vmem_limit_bytes=60 << 20),
-            **kw,
-        )(*args)
-
-    return run
-
-
-def k_relayout(v_ref, s_ref):
-    relayout(v_ref, s_ref)
-
-
-def k_beam(pos_ref, r1_ref, ah_ref, al_ref, b_ref, oh_ref):
-    fill_places(pos_ref, oh_ref)
-    beamform(oh_ref, r1_ref, ah_ref, al_ref, b_ref)
-
-
-def k_power(r2_ref, ch_ref, cl_ref, delay_ref, i_ref, z_ref, cc_ref, f_ref, tab_ref):
-    fill_spectrum(f_ref)
-    fill_trials(delay_ref, tab_ref)
-
-    def block(j, t, r):
-        return r2_ref[j, t % 2, t // 2, r]
-
-    power(block, ch_ref, cl_ref, i_ref, cc_ref)
-    dedisperse(f_ref, cc_ref, tab_ref, z_ref)
-
-
-def k_series(z_ref, o_ref, m_ref):
-    fill_inverse(m_ref)
-    zs = z_ref[0].astype(F32)
-    for k in range(1, 4):
-        zs = zs + z_ref[k].astype(F32)
-    series(zs, m_ref, o_ref)
+MESH = pl.DeviceIdType.MESH
+
+
+def kernel(
+    v_ref, pos_ref, delay_ref, ah_any, al_any, ch_any, cl_any,
+    i_ref, d_ref,
+    vbuf, ah, al, ch, cl, s1, r1, oh, hh, hl, b, r2, cc, f, tab, m, z, rx, zz, rz,
+    load, send1, recv1, send2, recv2, sendx, recvx, sendz, recvz,
+):
+    channel, tm, beam = lax.axis_index("channel"), lax.axis_index("tm"), lax.axis_index("beam")
+    z_hi, x, z_lo, core = channel >> 2, channel & 3, beam >> 1, beam & 1
+    place = z_hi * 4 + z_lo
+
+    loads = [
+        pltpu.make_async_copy(src, dst, load.at[n])
+        for n, (src, dst) in enumerate([(v_ref, vbuf), (ah_any, ah), (al_any, al), (ch_any, ch), (cl_any, cl)])
+    ]
+    for copy in loads:
+        copy.start()
+
+    def plane(act):
+        def around(to, dx, dc):
+            act(((to >> 2) << 2) + ((x + dx) & 3), ((to & 3) << 1) + ((core + dc) & 1))
+
+        def step(n, carry):
+            left = 15 - n
+            far = ((left + 1) >> 1) * (((left & 1) << 1) - 1)
+            to = (place + far + 16) & 15
+            for dx in range(4):
+                for dc in range(2):
+                    around(to, dx, dc)
+            return carry
+
+        lax.fori_loop(0, 15, step, 0)
+        for dx in range(4):
+            for dc in range(2):
+                if dx or dc:
+                    around(place, dx, dc)
+
+    barrier = pltpu.get_barrier_semaphore()
+
+    def greet(c, bm):
+        pl.semaphore_signal(barrier, inc=1, device_id={"channel": c, "tm": tm, "beam": bm}, device_id_type=MESH)
+
+    plane(greet)
+    for n in range(1, 4):
+        for bm in range(8):
+            pl.semaphore_signal(
+                barrier, inc=1, device_id={"channel": channel, "tm": (tm + n) & 3, "beam": bm}, device_id_type=MESH
+            )
+    loads[0].wait()
+    relayout(vbuf, s1)
+    fill_places(pos_ref, oh)
+    pl.semaphore_wait(barrier, 151)
+
+    def remote(src, dst, send, recv, c, t, bm):
+        return pltpu.make_async_remote_copy(
+            src_ref=src, dst_ref=dst, send_sem=send, recv_sem=recv,
+            device_id={"channel": c, "tm": t, "beam": bm}, device_id_type=MESH,
+        )
+
+    def bulk(src, dst, send, recv):
+        return remote(src, dst, send, recv, channel, tm, beam ^ 1)
+
+    feed = beam * 16 + channel
+    plane(lambda c, bm: remote(s1.at[c * 8 + bm], r1.at[feed], send1, recv1, c, tm, bm).start())
+    r1[feed] = s1[channel * 8 + beam]
+    fill_spectrum(f)
+    fill_trials(delay_ref, tab)
+    fill_inverse(m)
+    for copy in loads[1:]:
+        copy.wait()
+    first = bulk(s1.at[pl.ds(0, 127)], r1.at[pl.ds(0, 127)], send1, recv1)
+    first.wait_recv()
+
+    grid_sums(oh, r1, hh, hl)
+    slot = z_lo * 8 + tm * 2 + core
+    a_hi, a_lo = ah[...], al[...]
+
+    def pass_on(be, own):
+        for dc in range(2):
+            for dt in range(4):
+                if own and dc == 0 and dt == 0:
+                    continue
+                co, t = (core + dc) & 1, (tm + dt) & 3
+                remote(b.at[be * 8 + co * 4 + t], r2.at[slot], send2, recv2, channel, t, be * 2 + co).start()
+
+    east = [(z_lo + 3 - n) & 3 for n in range(4)]
+    for n in range(4):
+        north_beams(east[n], hh, hl, a_hi, a_lo, b)
+        if n:
+            pass_on(east[n - 1], False)
+    r2[slot] = b[z_lo * 8 + core * 4 + tm]
+    pass_on(z_lo, True)
+    second = bulk(b.at[pl.ds(0, 31)], r2.at[pl.ds(0, 31)], send2, recv2)
+    second.wait_recv()
+
+    power(lambda j, t, r: r2[j * 8 + t, r], ch, cl, i_ref, cc)
+
+    def to_x(q):
+        for n in range(1, 4):
+            to = (x + n) & 3
+            remote(z.at[q, to], rx.at[x, q], sendx.at[q // 4], recvx.at[q // 4], z_hi * 4 + to, tm, beam).start()
+
+    for q in range(8):
+        z[q] = bin_quad(q, f, cc, tab)
+        if q:
+            to_x(q - 1)
+            rx[x, q - 1] = z[q - 1, x]
+    rx[x, 7] = z[7, x]
+    to_x(7)
+
+    def to_z(half):
+        quads = pl.ds(half * 4, 4)
+        for n in range(1, 4):
+            to = (z_hi + n) & 3
+            remote(
+                zz.at[to, quads], rz.at[z_hi, quads], sendz.at[half], recvz.at[half], to * 4 + x, tm, beam
+            ).start()
+
+    def sums_x(half):
+        for q in range(half * 4, half * 4 + 4):
+            total = rx[0, q].astype(F32)
+            for n in range(1, 4):
+                total = total + rx[n, q].astype(F32)
+            zz[:, q] = total.astype(BF16).reshape(4, 16, 128)
+
+    x_copies = [bulk(rx.at[pl.ds(0, 3), pl.ds(0, 4)], rx.at[pl.ds(0, 3), pl.ds(0, 4)], sendx.at[n], recvx.at[n]) for n in range(2)]
+    z_copies = [bulk(zz.at[pl.ds(0, 3), pl.ds(0, 4)], rz.at[pl.ds(0, 3), pl.ds(0, 4)], sendz.at[n], recvz.at[n]) for n in range(2)]
+    for half in range(2):
+        x_copies[half].wait_recv()
+        sums_x(half)
+        rz[z_hi, pl.ds(half * 4, 4)] = zz[z_hi, pl.ds(half * 4, 4)]
+        to_z(half)
+    first.wait_send()
+    second.wait_send()
+    for half in range(2):
+        x_copies[half].wait_send()
+    for half in range(2):
+        z_copies[half].wait_recv()
+    total = rz[0].astype(F32)
+    for n in range(1, 4):
+        total = total + rz[n].astype(F32)
+    series(total.reshape(128, 128), m, d_ref)
+    for half in range(2):
+        z_copies[half].wait_send()
 
 
 def S(shape, dtype):
     return jax.ShapeDtypeStruct(shape, dtype)
 
 
-run_relayout = call(k_relayout, S((128, 32, 128), BF16))
-run_beam = call(k_beam, S((32, 2, 32, 128), BF16), [pltpu.VMEM((1024, FEEDS), BF16)])
-run_power = call(
-    k_power,
-    [S((1024, 128), F32), S((4, 64, 1024), BF16)],
-    [pltpu.VMEM((128, 1024), BF16), pltpu.VMEM((1024, 1024), BF16), pltpu.VMEM((8, 256, 512), BF16)],
-)
-run_series = call(k_series, S((256, 64), F32), [pltpu.VMEM((4, 128, 512), F32)])
-
-
 def per_device(voltages, positions, delays):
-    a_hi, a_lo = table_split(north_table())
-    c_hi, c_lo = table_split(filter_table())
-    s1 = run_relayout(voltages)
-    r1 = lax.all_to_all(s1, ("z_hi", "x", "z_lo", "core"), 0, 0, tiled=True)
-    pos = positions.reshape(8, 16, 16).swapaxes(0, 1).reshape(1, FEEDS)
-    b = run_beam(pos, r1, a_hi, a_lo)
-    r2 = lax.all_to_all(b, ("z_lo", "core", "tm"), 0, 0, tiled=True)
-    i, z = run_power(r2.reshape(4, 2, 4, 2, 32, 128), c_hi, c_lo, delays.T)
-    z = lax.all_to_all(z, "x", 0, 0, tiled=True)
-    z = z.astype(F32).sum(axis=0).astype(BF16).reshape(4, 16, 1024)
-    z = lax.all_to_all(z, "z_hi", 0, 0, tiled=True)
-    d = run_series(z)
+    tables = table_split(north_table()) + table_split(filter_table())
+    vmem = pl.BlockSpec(memory_space=pltpu.VMEM)
+    hbm = pl.BlockSpec(memory_space=pl.ANY)
+    V = pltpu.VMEM
+    dma = pltpu.SemaphoreType.DMA
+    i, d = pl.pallas_call(
+        kernel,
+        out_shape=[S((1024, 128), F32), S((256, 64), F32)],
+        in_specs=[hbm, vmem, vmem] + [hbm] * 4,
+        out_specs=[vmem, vmem],
+        scratch_shapes=[
+            V((2, 16, 64, 256), BF16),
+            V((256, 512), BF16),
+            V((256, 512), BF16),
+            V((512, 256), BF16),
+            V((512, 256), BF16),
+            V((128, 32, 128), BF16),
+            V((128, 32, 128), BF16),
+            V((1024, FEEDS), BF16),
+            V((4, 512, 256), BF16),
+            V((4, 512, 256), BF16),
+            V((32, 2, 32, 128), BF16),
+            V((32, 2, 32, 128), BF16),
+            V((128, 1024), BF16),
+            V((1024, 1024), BF16),
+            V((8, 256, 512), BF16),
+            V((4, 128, 512), F32),
+            V((8, 4, 64, 128), BF16),
+            V((4, 8, 64, 128), BF16),
+            V((4, 8, 16, 128), BF16),
+            V((4, 8, 16, 128), BF16),
+            dma((5,)),
+            dma,
+            dma,
+            dma,
+            dma,
+            dma((2,)),
+            dma((2,)),
+            dma((2,)),
+            dma((2,)),
+        ],
+        compiler_params=pltpu.CompilerParams(collective_id=0, has_side_effects=True, vmem_limit_bytes=60 << 20),
+    )(voltages, positions.reshape(1, FEEDS), delays.T, *tables)
     i = i.reshape(32, 8, 4, 128).swapaxes(1, 2).reshape(32, 4, 1024)
     return i, d.reshape(32, 8, 64)
 
 
 def solution(mesh):
-    finer = Mesh(mesh.devices.reshape(4, 4, 4, 4, 2), ("z_hi", "x", "tm", "z_lo", "core"))
-    beam, channel = ("z_lo", "core"), ("z_hi", "x")
+    beam = ("beam", "tm")
     return jax.shard_map(
         per_device,
-        mesh=finer,
-        in_specs=(P(None, beam + channel, None, "tm"), P(), P(None, channel)),
-        out_specs=(P(beam + ("tm",), channel, None), P(beam + ("tm",), channel, None)),
+        mesh=mesh,
+        in_specs=(P(None, ("beam", "channel"), None, "tm"), P(), P(None, "channel")),
+        out_specs=(P(beam, "channel", None), P(beam, "channel", None)),
         check_vma=False,
     )

time: 155 us -> 105 us (0.68); the launches traced: 153 us -> 105 us
  Pallas kernels: 22.4 us -> 102 us
  waiting for transfers between devices: 55.1 us -> 0 us
  blocking collectives: 52.9 us -> 0 us
  starting transfers between devices: 20.5 us -> 0 us
    pallas_call x4 -> x1, Pallas kernels: 22.4 us -> 102 us  [per_device(): pl.pallas_call(kernel, out_shape=[S((1024, 128), F32), S((256, 64), F32)]...]
    all_to_all x1 -> x0, waiting for transfers between devices: 55.1 us -> none  [per_device(): r1 = lax.all_to_all(s1, ('z_hi', 'x', 'z_lo', 'core'), 0, 0, tiled=True)]
    all_to_all x3 -> x0, blocking collectives: 52.9 us -> none  [the longest x1 23.8 us: per_device(): r2 = lax.all_to_all(b, ('z_lo', 'core', 'tm'), 0, 0, tiled=True)]
    all_to_all x1 -> x0, starting transfers between devices: 20.5 us -> none  [per_device(): r1 = lax.all_to_all(s1, ('z_hi', 'x', 'z_lo', 'core'), 0, 0, tiled=True)]
    unnamed x4, local copies, waits for them, and re-layouts: 0.98 us -> 2.56 us
  transfers between devices with their start and end apart: 1 -> 0, of which waited for: 1 -> 0; matrix products, arithmetic and copies ran while one was open for 1% -> 0% of each run, Pallas kernels for 0% -> 0%
where the time goes in v2:
time: 105 us
  Pallas kernels  102 us (97%)
  local copies, waits for them, and re-layouts  2.56 us (2%)
    pallas_call x1, Pallas kernels, per_device(): pl.pallas_call(kernel, out_shape=[S((1024, 128), F32), S((256, 64), F32)]...  102 us
    unnamed x4, local copies, waits for them, and re-layouts  2.56 us

profile of v2, /device:TPU:1, one launch (start us, length us, event | category | flops | bytes accessed | tf_op | source)
XLA Modules:
  0.0 105.0 jit_solution(2692805808229948103)
XLA Ops:
  0.6 101.8 %shard_map.68 = (f32[1024,128]{1,0:T(8,128)}, f32[256,64]{1,0:T(8,128)}) custom-call(bf16[2,16,64,256]{3,2,1,0:T(8,128)(2,1)} %v_ref.1, s32[1,2048]{1,0:T(1,128)} %bitcast.11, s32[64,128]{1,0:T(8,128)} %bitcast.10, bf16[256,512]{1,0:T(8,128)(2,1)} %constant.7.ah_any, bf16[256,512]{1,0:T(8,128)(2,1)} %constant.10.al_any, bf16[512,256]{1,0:T(8,128)(2,1)} %constant.11.ch_any, ...), custom_call_target="tpu_custom_call" | custom-call | tf_op jit(solution)/shard_map/pallas_call | solution.py:372
  102.4 0.0 copy-start
  102.4 1.9 %copy.10 = f32[32,4,1024]{2,1,0:T(4,128)} copy(f32[32,4,1024]{2,1,0:T(4,128)} %bitcast.8) | data formatting | bytes 1048576
  104.3 0.0 copy-done
  104.3 0.7 copy.11
Async XLA Ops:
  102.4 1.9 %copy-start = (f32[256,64]{1,0:T(8,128)S(1)}, f32[256,64]{1,0:T(8,128)}, u32[]{:S(2)}) copy-start(f32[256,64]{1,0:T(8,128)} %get-tuple-element.5) | copy-start | bytes 196612

commit v3 on v2

--- a/solution.py
+++ b/solution.py
@@ -15,6 +15,8 @@
 UPCH = 16
 FRAMES = 64
 FINE = 1024
+PIECES = 4
+QUADS = 8 // PIECES
 
 
 def cos_turns(steps, period):
@@ -151,7 +153,7 @@
     lax.fori_loop(0, 8, body, start)
 
 
-def fill_inverse(m_ref):
+def fill_inverse(mh_ref, ml_ref):
     for w4 in range(4):
         row = lax.broadcasted_iota(jnp.int32, (128, 512), 0)
         lane = lax.broadcasted_iota(jnp.int32, (128, 512), 1)
@@ -159,7 +161,7 @@
         steps = w * (lane & 63) + ((row >> 3) & 1) * 16
         value = jnp.where((row & 7) == (lane >> 6), cos_turns(steps, 64), 0.0)
         scale = jnp.where(w == FRAMES // 2, 1.0, 2.0) * (1.0 / (FRAMES * math.sqrt(FINE)))
-        m_ref[w4] = value * scale
+        mh_ref[w4], ml_ref[w4] = split(value * scale)
 
 
 def power(block, c_hi_ref, c_lo_ref, out_ref, cc_ref):
@@ -200,13 +202,12 @@
     return mm(tab_ref[q], right).astype(BF16).reshape(4, 64, 128)
 
 
-def series(v, m_ref, out_ref):
-    vt = jnp.transpose(v)
+def series(v, mh_ref, ml_ref, out_ref):
+    v_hi, v_lo = split(jnp.transpose(v))
     res = jnp.zeros((32, 512), F32)
     for w4 in range(4):
-        res = res + jnp.dot(
-            vt[w4 * 32 : w4 * 32 + 32], m_ref[w4], precision=lax.Precision.HIGHEST, preferred_element_type=F32
-        )
+        rows = slice(w4 * 32, w4 * 32 + 32)
+        res = res + mm(v_hi[rows], mh_ref[w4]) + (mm(v_lo[rows], mh_ref[w4]) + mm(v_hi[rows], ml_ref[w4]))
     for d in range(8):
         out_ref[pl.ds(d, 32, stride=8), :] = res[:, d * 64 : d * 64 + 64]
 
@@ -216,9 +217,9 @@
 
 def kernel(
     v_ref, pos_ref, delay_ref, ah_any, al_any, ch_any, cl_any,
-    i_ref, d_ref,
-    vbuf, ah, al, ch, cl, s1, r1, oh, hh, hl, b, r2, cc, f, tab, m, z, rx, zz, rz,
-    load, send1, recv1, send2, recv2, sendx, recvx, sendz, recvz,
+    i_out, d_ref,
+    i_ref, vbuf, ah, al, ch, cl, s1, r1, oh, hh, hl, b, r2, cc, f, tab, mh, ml, z, rx, zz, rz,
+    load, send1, recv1, send2, recv2, sendx, recvx, sendz, recvz, wave,
 ):
     channel, tm, beam = lax.axis_index("channel"), lax.axis_index("tm"), lax.axis_index("beam")
     z_hi, x, z_lo, core = channel >> 2, channel & 3, beam >> 1, beam & 1
@@ -231,40 +232,46 @@
     for copy in loads:
         copy.start()
 
-    def plane(act):
-        def around(to, dx, dc):
-            act(((to >> 2) << 2) + ((x + dx) & 3), ((to & 3) << 1) + ((core + dc) & 1))
-
+    def around(to, act):
+        for dx in range(4):
+            for dc in range(2):
+                act(((to >> 2) << 2) + ((x + dx) & 3), ((to & 3) << 1) + ((core + dc) & 1))
+
+    def rings(first, count, act):
         def step(n, carry):
-            left = 15 - n
+            left = first - n
             far = ((left + 1) >> 1) * (((left & 1) << 1) - 1)
-            to = (place + far + 16) & 15
-            for dx in range(4):
-                for dc in range(2):
-                    around(to, dx, dc)
+            around((place + far + 16) & 15, act)
             return carry
 
-        lax.fori_loop(0, 15, step, 0)
+        lax.fori_loop(0, count, step, 0)
+
+    def here(act):
         for dx in range(4):
             for dc in range(2):
                 if dx or dc:
-                    around(place, dx, dc)
+                    act((z_hi << 2) + ((x + dx) & 3), (z_lo << 1) + ((core + dc) & 1))
 
     barrier = pltpu.get_barrier_semaphore()
 
     def greet(c, bm):
         pl.semaphore_signal(barrier, inc=1, device_id={"channel": c, "tm": tm, "beam": bm}, device_id_type=MESH)
 
-    plane(greet)
+    rings(8, 8, greet)
     for n in range(1, 4):
         for bm in range(8):
             pl.semaphore_signal(
                 barrier, inc=1, device_id={"channel": channel, "tm": (tm + n) & 3, "beam": bm}, device_id_type=MESH
             )
+    here(greet)
     loads[0].wait()
     relayout(vbuf, s1)
-    fill_places(pos_ref, oh)
-    pl.semaphore_wait(barrier, 151)
+    pl.semaphore_wait(barrier, 95)
+    for n, turn in ((0, 1), (1, 3)):
+        to = ((z_hi + turn) & 3) * 4 + x
+        pl.semaphore_signal(
+            wave.at[n], inc=1, device_id={"channel": to, "tm": tm, "beam": beam}, device_id_type=MESH
+        )
 
     def remote(src, dst, send, recv, c, t, bm):
         return pltpu.make_async_remote_copy(
@@ -276,11 +283,21 @@
         return remote(src, dst, send, recv, channel, tm, beam ^ 1)
 
     feed = beam * 16 + channel
-    plane(lambda c, bm: remote(s1.at[c * 8 + bm], r1.at[feed], send1, recv1, c, tm, bm).start())
+
+    def hand(c, bm):
+        remote(s1.at[c * 8 + bm], r1.at[feed], send1, recv1, c, tm, bm).start()
+
+    rings(6, 2, hand)
+    pl.semaphore_wait(wave.at[0], 1)
+    pl.semaphore_wait(wave.at[1], 1)
+    rings(15, 9, hand)
+    rings(4, 4, hand)
+    here(hand)
     r1[feed] = s1[channel * 8 + beam]
+    fill_places(pos_ref, oh)
     fill_spectrum(f)
     fill_trials(delay_ref, tab)
-    fill_inverse(m)
+    fill_inverse(mh, ml)
     for copy in loads[1:]:
         copy.wait()
     first = bulk(s1.at[pl.ds(0, 127)], r1.at[pl.ds(0, 127)], send1, recv1)
@@ -310,10 +327,13 @@
 
     power(lambda j, t, r: r2[j * 8 + t, r], ch, cl, i_ref, cc)
 
+    kept = pltpu.make_async_copy(i_ref, i_out, load.at[5])
+    kept.start()
+
     def to_x(q):
         for n in range(1, 4):
             to = (x + n) & 3
-            remote(z.at[q, to], rx.at[x, q], sendx.at[q // 4], recvx.at[q // 4], z_hi * 4 + to, tm, beam).start()
+            remote(z.at[q, to], rx.at[x, q], sendx.at[q // QUADS], recvx.at[q // QUADS], z_hi * 4 + to, tm, beam).start()
 
     for q in range(8):
         z[q] = bin_quad(q, f, cc, tab)
@@ -323,44 +343,59 @@
     rx[x, 7] = z[7, x]
     to_x(7)
 
-    def to_z(half):
-        quads = pl.ds(half * 4, 4)
+    def to_z(piece):
+        quads = pl.ds(piece * QUADS, QUADS)
         for n in range(1, 4):
             to = (z_hi + n) & 3
             remote(
-                zz.at[to, quads], rz.at[z_hi, quads], sendz.at[half], recvz.at[half], to * 4 + x, tm, beam
+                zz.at[to, quads], rz.at[z_hi, quads], sendz.at[piece], recvz.at[piece], to * 4 + x, tm, beam
             ).start()
 
-    def sums_x(half):
-        for q in range(half * 4, half * 4 + 4):
+    def sums_x(piece):
+        for q in range(piece * QUADS, piece * QUADS + QUADS):
             total = rx[0, q].astype(F32)
             for n in range(1, 4):
                 total = total + rx[n, q].astype(F32)
             zz[:, q] = total.astype(BF16).reshape(4, 16, 128)
 
-    x_copies = [bulk(rx.at[pl.ds(0, 3), pl.ds(0, 4)], rx.at[pl.ds(0, 3), pl.ds(0, 4)], sendx.at[n], recvx.at[n]) for n in range(2)]
-    z_copies = [bulk(zz.at[pl.ds(0, 3), pl.ds(0, 4)], rz.at[pl.ds(0, 3), pl.ds(0, 4)], sendz.at[n], recvz.at[n]) for n in range(2)]
-    for half in range(2):
-        x_copies[half].wait_recv()
-        sums_x(half)
-        rz[z_hi, pl.ds(half * 4, 4)] = zz[z_hi, pl.ds(half * 4, 4)]
-        to_z(half)
+    x_copies = [bulk(rx.at[pl.ds(0, 3), pl.ds(0, QUADS)], rx.at[pl.ds(0, 3), pl.ds(0, QUADS)], sendx.at[n], recvx.at[n]) for n in range(PIECES)]
+    z_copies = [bulk(zz.at[pl.ds(0, 3), pl.ds(0, QUADS)], rz.at[pl.ds(0, 3), pl.ds(0, QUADS)], sendz.at[n], recvz.at[n]) for n in range(PIECES)]
+    for piece in range(PIECES):
+        x_copies[piece].wait_recv()
+        sums_x(piece)
+        rz[z_hi, pl.ds(piece * QUADS, QUADS)] = zz[z_hi, pl.ds(piece * QUADS, QUADS)]
+        to_z(piece)
+    kept.wait()
     first.wait_send()
     second.wait_send()
-    for half in range(2):
-        x_copies[half].wait_send()
-    for half in range(2):
-        z_copies[half].wait_recv()
+    for piece in range(PIECES):
+        x_copies[piece].wait_send()
+    for piece in range(PIECES):
+        z_copies[piece].wait_recv()
     total = rz[0].astype(F32)
     for n in range(1, 4):
         total = total + rz[n].astype(F32)
-    series(total.reshape(128, 128), m, d_ref)
-    for half in range(2):
-        z_copies[half].wait_send()
+    series(total.reshape(128, 128), mh, ml, d_ref)
+    for piece in range(PIECES):
+        z_copies[piece].wait_send()
 
 
 def S(shape, dtype):
     return jax.ShapeDtypeStruct(shape, dtype)
+
+
+def put_out(i_ref, d_ref, i_out, d_out, i_buf, d_buf, sems):
+    pairs = [(i_ref.at[pl.ds(n * 256, 256)], i_buf.at[pl.ds(n * 256, 256)], i_out.at[pl.ds(n * 256, 256)]) for n in range(4)]
+    pairs.append((d_ref, d_buf, d_out))
+    come = [pltpu.make_async_copy(a, b, sems.at[0, n]) for n, (a, b, c) in enumerate(pairs)]
+    go = [pltpu.make_async_copy(b, c, sems.at[1, n]) for n, (a, b, c) in enumerate(pairs)]
+    for copy in come:
+        copy.start()
+    for n in range(5):
+        come[n].wait()
+        go[n].start()
+    for copy in go:
+        copy.wait()
 
 
 def per_device(voltages, positions, delays):
@@ -373,8 +408,9 @@
         kernel,
         out_shape=[S((1024, 128), F32), S((256, 64), F32)],
         in_specs=[hbm, vmem, vmem] + [hbm] * 4,
-        out_specs=[vmem, vmem],
+        out_specs=[hbm, vmem],
         scratch_shapes=[
+            V((1024, 128), F32),
             V((2, 16, 64, 256), BF16),
             V((256, 512), BF16),
             V((256, 512), BF16),
@@ -390,23 +426,32 @@
             V((128, 1024), BF16),
             V((1024, 1024), BF16),
             V((8, 256, 512), BF16),
-            V((4, 128, 512), F32),
+            V((4, 128, 512), BF16),
+            V((4, 128, 512), BF16),
             V((8, 4, 64, 128), BF16),
             V((4, 8, 64, 128), BF16),
             V((4, 8, 16, 128), BF16),
             V((4, 8, 16, 128), BF16),
-            dma((5,)),
+            dma((6,)),
             dma,
             dma,
             dma,
             dma,
-            dma((2,)),
-            dma((2,)),
-            dma((2,)),
-            dma((2,)),
+            dma((PIECES,)),
+            dma((PIECES,)),
+            dma((PIECES,)),
+            dma((PIECES,)),
+            pltpu.SemaphoreType.REGULAR((2,)),
         ],
         compiler_params=pltpu.CompilerParams(collective_id=0, has_side_effects=True, vmem_limit_bytes=60 << 20),
     )(voltages, positions.reshape(1, FEEDS), delays.T, *tables)
+    i, d = pl.pallas_call(
+        put_out,
+        out_shape=[S((1024, 128), F32), S((256, 64), F32)],
+        in_specs=[hbm, hbm],
+        out_specs=[hbm, hbm],
+        scratch_shapes=[V((1024, 128), F32), V((256, 64), F32), dma((2, 5))],
+    )(i, d)
     i = i.reshape(32, 8, 4, 128).swapaxes(1, 2).reshape(32, 4, 1024)
     return i, d.reshape(32, 8, 64)
 

time: 105 us -> 103 us (0.981)
  local copies, waits for them, and re-layouts: 2.56 us -> 0 us
    unnamed x4 -> x0, local copies, waits for them, and re-layouts: 2.56 us -> none
    pallas_call x0 -> x1, Pallas kernels: none -> 1.91 us  [per_device(): pl.pallas_call(put_out, out_shape=[S((1024, 128), F32), S((256, 64), F32)...]
    pallas_call x1, Pallas kernels: 102 us -> 100 us  [per_device(): pl.pallas_call(kernel, out_shape=[S((1024, 128), F32), S((256, 64), F32)]...]
where the time goes in v3:
time: 103 us
  Pallas kernels  102 us (99%)
    pallas_call x1, Pallas kernels, per_device(): pl.pallas_call(kernel, out_shape=[S((1024, 128), F32), S((256, 64), F32)]...  100 us

profile of v3, /device:TPU:1, one launch (start us, length us, event | category | flops | bytes accessed | tf_op | source)
XLA Modules:
  0.0 103.0 jit_solution(12627197285530962927)
XLA Ops:
  0.6 100.5 %shard_map.68 = (f32[1024,128]{1,0:T(8,128)}, f32[256,64]{1,0:T(8,128)}) custom-call(bf16[2,16,64,256]{3,2,1,0:T(8,128)(2,1)} %v_ref.1, s32[1,2048]{1,0:T(1,128)} %bitcast.9, s32[64,128]{1,0:T(8,128)} %bitcast.8, bf16[256,512]{1,0:T(8,128)(2,1)} %constant.7.ah_any, bf16[256,512]{1,0:T(8,128)(2,1)} %constant.10.al_any, bf16[512,256]{1,0:T(8,128)(2,1)} %constant.11.ch_any, ...), custom_call_target="tpu_custom_call" | custom-call | tf_op jit(solution)/shard_map/pallas_call | solution.py:407
  101.1 1.9 %shard_map.69 = (f32[1024,128]{1,0:T(8,128)}, f32[256,64]{1,0:T(8,128)}) custom-call(f32[1024,128]{1,0:T(8,128)} %get-tuple-element.6.i_ref, f32[256,64]{1,0:T(8,128)} %get-tuple-element.7.d_ref), custom_call_target="tpu_custom_call" | custom-call | tf_op jit(solution)/shard_map/pallas_call | solution.py:448

commit v4 on v3

--- a/solution.py
+++ b/solution.py
@@ -15,8 +15,6 @@
 UPCH = 16
 FRAMES = 64
 FINE = 1024
-PIECES = 4
-QUADS = 8 // PIECES
 
 
 def cos_turns(steps, period):
@@ -137,7 +135,7 @@
     dd = jnp.concatenate([dt, dt], axis=1)
     rows = []
     for rb in range(32):
-        d = ((rb // 2) % 4) * 4 + rb // 8
+        d = (rb // 8) * 4 + (rb // 2) % 4
         rows.append(dd[d * 8 : d * 8 + 8, :])
     step = jnp.concatenate(rows, axis=0)
     row = lax.broadcasted_iota(jnp.int32, (256, 128), 0)
@@ -164,28 +162,26 @@
         mh_ref[w4], ml_ref[w4] = split(value * scale)
 
 
-def power(block, c_hi_ref, c_lo_ref, out_ref, cc_ref):
-    c_hi, c_lo = c_hi_ref[...], c_lo_ref[...]
+def power(j, block, c_hi_ref, c_lo_ref, out_ref, cc_ref):
     zero = jnp.zeros((32, 128), BF16)
-    for j in range(4):
-        cur = [jnp.concatenate([block(j, t, r) for t in range(8)], axis=0) for r in range(2)]
-        old = [jnp.concatenate([zero, cur[r][:224]], axis=0) for r in range(2)]
-        left = jnp.concatenate(old + cur, axis=1)
-        y = mm(left, c_hi) + mm(left, c_lo)
-        p = y[:, :128] * y[:, :128] + y[:, 128:] * y[:, 128:]
-        total = p[0:32]
-        for t in range(1, 8):
-            total = total + p[t * 32 : t * 32 + 32]
-        for shift in (16, 32, 64):
-            total = total + pltpu.roll(total, shift, 1)
-        mean = total * (1.0 / FRAMES)
-        for t in range(8):
-            pt = p[t * 32 : t * 32 + 32]
-            out_ref[pl.ds(t * 4 + j, 32, stride=32), :] = pt
-            cc_ref[j * 32 : j * 32 + 32, t * 128 : t * 128 + 128] = (pt - mean).astype(BF16)
-
-
-def bin_quad(q, f_ref, cc_ref, tab_ref):
+    cur = [jnp.concatenate([block(t, r) for t in range(8)], axis=0) for r in range(2)]
+    old = [jnp.concatenate([zero, cur[r][:224]], axis=0) for r in range(2)]
+    left = jnp.concatenate(old + cur, axis=1)
+    y = mm(left, c_hi_ref[...]) + mm(left, c_lo_ref[...])
+    p = y[:, :128] * y[:, :128] + y[:, 128:] * y[:, 128:]
+    total = p[0:32]
+    for t in range(1, 8):
+        total = total + p[t * 32 : t * 32 + 32]
+    for shift in (16, 32, 64):
+        total = total + pltpu.roll(total, shift, 1)
+    mean = total * (1.0 / FRAMES)
+    for t in range(8):
+        pt = p[t * 32 : t * 32 + 32]
+        out_ref[pl.ds(t * 4 + j, 32, stride=32), :] = pt
+        cc_ref[pl.ds(pl.multiple_of(j * 32, 32), 32), t * 128 : t * 128 + 128] = (pt - mean).astype(BF16)
+
+
+def bin_quad(q, f_ref, cc_ref):
     group = lax.broadcasted_iota(jnp.int32, (16, 128), 1) >> 5
     s = lax.dot_general(
         f_ref[q * 128 : q * 128 + 128, :], cc_ref[...], (((1,), (1,)), ((), ())), preferred_element_type=F32
@@ -198,8 +194,7 @@
                 at = (w4 * 2 + r) * 16
                 part = turned[(w4 - j) % 4][at : at + 16]
                 rows.append(jnp.where(group == w4, part, 0.0).astype(BF16))
-    right = jnp.concatenate(rows, axis=0)
-    return mm(tab_ref[q], right).astype(BF16).reshape(4, 64, 128)
+    return jnp.concatenate(rows, axis=0)
 
 
 def series(v, mh_ref, ml_ref, out_ref):
@@ -218,7 +213,7 @@
 def kernel(
     v_ref, pos_ref, delay_ref, ah_any, al_any, ch_any, cl_any,
     i_out, d_ref,
-    i_ref, vbuf, ah, al, ch, cl, s1, r1, oh, hh, hl, b, r2, cc, f, tab, mh, ml, z, rx, zz, rz,
+    i_ref, vbuf, ah, al, ch, cl, s1, r1, oh, hh, hl, b, r2, cc, f, tab, right, mh, ml, z, rx, zz, rz,
     load, send1, recv1, send2, recv2, sendx, recvx, sendz, recvz, wave,
 ):
     channel, tm, beam = lax.axis_index("channel"), lax.axis_index("tm"), lax.axis_index("beam")
@@ -307,77 +302,70 @@
     slot = z_lo * 8 + tm * 2 + core
     a_hi, a_lo = ah[...], al[...]
 
-    def pass_on(be, own):
+    def pass_on(n):
+        be, own = east[n], n == 3
         for dc in range(2):
             for dt in range(4):
                 if own and dc == 0 and dt == 0:
                     continue
                 co, t = (core + dc) & 1, (tm + dt) & 3
-                remote(b.at[be * 8 + co * 4 + t], r2.at[slot], send2, recv2, channel, t, be * 2 + co).start()
+                remote(b.at[be * 8 + co * 4 + t], r2.at[slot], send2, recv2.at[(n + 1) & 3], channel, t, be * 2 + co).start()
 
     east = [(z_lo + 3 - n) & 3 for n in range(4)]
     for n in range(4):
         north_beams(east[n], hh, hl, a_hi, a_lo, b)
         if n:
-            pass_on(east[n - 1], False)
+            pass_on(n - 1)
     r2[slot] = b[z_lo * 8 + core * 4 + tm]
-    pass_on(z_lo, True)
-    second = bulk(b.at[pl.ds(0, 31)], r2.at[pl.ds(0, 31)], send2, recv2)
-    second.wait_recv()
-
-    power(lambda j, t, r: r2[j * 8 + t, r], ch, cl, i_ref, cc)
+    pass_on(3)
+    for n in (1, 2, 3, 0):
+        j = (z_lo + n) & 3
+        count = 8 if n else 7
+        bulk(b.at[pl.ds(0, count)], r2.at[pl.ds(0, count)], send2, recv2.at[n]).wait_recv()
+        power(j, lambda t, r, j=j: r2[j * 8 + t, r], ch, cl, i_ref, cc)
 
     kept = pltpu.make_async_copy(i_ref, i_out, load.at[5])
     kept.start()
 
-    def to_x(q):
-        for n in range(1, 4):
-            to = (x + n) & 3
-            remote(z.at[q, to], rx.at[x, q], sendx.at[q // QUADS], recvx.at[q // QUADS], z_hi * 4 + to, tm, beam).start()
-
     for q in range(8):
-        z[q] = bin_quad(q, f, cc, tab)
-        if q:
-            to_x(q - 1)
-            rx[x, q - 1] = z[q - 1, x]
-    rx[x, 7] = z[7, x]
-    to_x(7)
-
-    def to_z(piece):
-        quads = pl.ds(piece * QUADS, QUADS)
-        for n in range(1, 4):
-            to = (z_hi + n) & 3
-            remote(
-                zz.at[to, quads], rz.at[z_hi, quads], sendz.at[piece], recvz.at[piece], to * 4 + x, tm, beam
-            ).start()
-
-    def sums_x(piece):
-        for q in range(piece * QUADS, piece * QUADS + QUADS):
-            total = rx[0, q].astype(F32)
-            for n in range(1, 4):
-                total = total + rx[n, q].astype(F32)
-            zz[:, q] = total.astype(BF16).reshape(4, 16, 128)
-
-    x_copies = [bulk(rx.at[pl.ds(0, 3), pl.ds(0, QUADS)], rx.at[pl.ds(0, 3), pl.ds(0, QUADS)], sendx.at[n], recvx.at[n]) for n in range(PIECES)]
-    z_copies = [bulk(zz.at[pl.ds(0, 3), pl.ds(0, QUADS)], rz.at[pl.ds(0, 3), pl.ds(0, QUADS)], sendz.at[n], recvz.at[n]) for n in range(PIECES)]
-    for piece in range(PIECES):
-        x_copies[piece].wait_recv()
-        sums_x(piece)
-        rz[z_hi, pl.ds(piece * QUADS, QUADS)] = zz[z_hi, pl.ds(piece * QUADS, QUADS)]
-        to_z(piece)
+        right[q] = bin_quad(q, f, cc)
+    turns = (2, 1, 3, 0)
+    for n in range(4):
+        to_z = (z_hi + turns[n]) & 3
+        rows = pl.ds(pl.multiple_of(to_z * 64, 64), 64)
+        for q in range(8):
+            z[to_z, :, q] = mm(tab[q, rows, :], right[q]).astype(BF16).reshape(4, 16, 128)
+        rx[to_z, x] = z[to_z, x]
+        for k in range(1, 4):
+            to = (x + k) & 3
+            remote(z.at[to_z, to], rx.at[to_z, x], sendx.at[n], recvx.at[n], z_hi * 4 + to, tm, beam).start()
+
+    x_copies = [bulk(z.at[0, pl.ds(0, 3)], rx.at[0, pl.ds(0, 3)], sendx.at[n], recvx.at[n]) for n in range(4)]
+    z_copies = [bulk(zz.at[0], rz.at[0], sendz.at[n], recvz.at[n]) for n in range(3)]
+    for n in range(4):
+        to_z = (z_hi + turns[n]) & 3
+        x_copies[n].wait_recv()
+        total = rx[to_z, 0].astype(F32)
+        for k in range(1, 4):
+            total = total + rx[to_z, k].astype(F32)
+        if n < 3:
+            zz[to_z] = total.astype(BF16)
+            remote(zz.at[to_z], rz.at[z_hi], sendz.at[n], recvz.at[n], to_z * 4 + x, tm, beam).start()
+        else:
+            rz[z_hi] = total.astype(BF16)
     kept.wait()
     first.wait_send()
-    second.wait_send()
-    for piece in range(PIECES):
-        x_copies[piece].wait_send()
-    for piece in range(PIECES):
-        z_copies[piece].wait_recv()
+    bulk(b.at[pl.ds(0, 31)], r2.at[pl.ds(0, 31)], send2, recv2.at[0]).wait_send()
+    for copy in x_copies:
+        copy.wait_send()
+    for copy in z_copies:
+        copy.wait_recv()
     total = rz[0].astype(F32)
     for n in range(1, 4):
         total = total + rz[n].astype(F32)
     series(total.reshape(128, 128), mh, ml, d_ref)
-    for piece in range(PIECES):
-        z_copies[piece].wait_send()
+    for copy in z_copies:
+        copy.wait_send()
 
 
 def S(shape, dtype):
@@ -426,21 +414,22 @@
             V((128, 1024), BF16),
             V((1024, 1024), BF16),
             V((8, 256, 512), BF16),
+            V((8, 512, 128), BF16),
             V((4, 128, 512), BF16),
             V((4, 128, 512), BF16),
-            V((8, 4, 64, 128), BF16),
-            V((4, 8, 64, 128), BF16),
+            V((4, 4, 8, 16, 128), BF16),
+            V((4, 4, 8, 16, 128), BF16),
             V((4, 8, 16, 128), BF16),
             V((4, 8, 16, 128), BF16),
             dma((6,)),
             dma,
             dma,
             dma,
-            dma,
-            dma((PIECES,)),
-            dma((PIECES,)),
-            dma((PIECES,)),
-            dma((PIECES,)),
+            dma((4,)),
+            dma((4,)),
+            dma((4,)),
+            dma((4,)),
+            dma((4,)),
             pltpu.SemaphoreType.REGULAR((2,)),
         ],
         compiler_params=pltpu.CompilerParams(collective_id=0, has_side_effects=True, vmem_limit_bytes=60 << 20),

time: 103 us -> 103 us (level)
  no operation moved by 1% of the time
where the time goes in v4:
time: 103 us; the launch traced here: 102 us
  Pallas kernels  102 us (99%)
    pallas_call x1, Pallas kernels, per_device(): pl.pallas_call(kernel, out_shape=[S((1024, 128), F32), S((256, 64), F32)]...  99.9 us

profile of v4, /device:TPU:1, one launch (start us, length us, event | category | flops | bytes accessed | tf_op | source)
XLA Modules:
  0.0 102.5 jit_solution(6410532719765196752)
XLA Ops:
  0.6 99.9 %shard_map.68 = (f32[1024,128]{1,0:T(8,128)}, f32[256,64]{1,0:T(8,128)}) custom-call(bf16[2,16,64,256]{3,2,1,0:T(8,128)(2,1)} %v_ref.1, s32[1,2048]{1,0:T(1,128)} %bitcast.9, s32[64,128]{1,0:T(8,128)} %bitcast.8, bf16[256,512]{1,0:T(8,128)(2,1)} %constant.7.ah_any, bf16[256,512]{1,0:T(8,128)(2,1)} %constant.10.al_any, bf16[512,256]{1,0:T(8,128)(2,1)} %constant.11.ch_any, ...), custom_call_target="tpu_custom_call" | custom-call | tf_op jit(solution)/shard_map/pallas_call | solution.py:395
  100.6 1.9 %shard_map.69 = (f32[1024,128]{1,0:T(8,128)}, f32[256,64]{1,0:T(8,128)}) custom-call(f32[1024,128]{1,0:T(8,128)} %get-tuple-element.6.i_ref, f32[256,64]{1,0:T(8,128)} %get-tuple-element.7.d_ref), custom_call_target="tpu_custom_call" | custom-call | tf_op jit(solution)/shard_map/pallas_call | solution.py:437

commit v5 on v4

--- a/solution.py
+++ b/solution.py
@@ -282,11 +282,11 @@
     def hand(c, bm):
         remote(s1.at[c * 8 + bm], r1.at[feed], send1, recv1, c, tm, bm).start()
 
-    rings(6, 2, hand)
+    rings(6, 4, hand)
     pl.semaphore_wait(wave.at[0], 1)
     pl.semaphore_wait(wave.at[1], 1)
     rings(15, 9, hand)
-    rings(4, 4, hand)
+    rings(2, 2, hand)
     here(hand)
     r1[feed] = s1[channel * 8 + beam]
     fill_places(pos_ref, oh)

time: 103 us -> 103 us (level)
  no operation moved by 1% of the time
where the time goes in v5:
time: 103 us
  Pallas kernels  102 us (99%)
    pallas_call x1, Pallas kernels, per_device(): pl.pallas_call(kernel, out_shape=[S((1024, 128), F32), S((256, 64), F32)]...  100 us

profile of v5, /device:TPU:1, one launch (start us, length us, event | category | flops | bytes accessed | tf_op | source)
XLA Modules:
  0.0 102.6 jit_solution(12919972026742090692)
XLA Ops:
  0.6 100.0 %shard_map.68 = (f32[1024,128]{1,0:T(8,128)}, f32[256,64]{1,0:T(8,128)}) custom-call(bf16[2,16,64,256]{3,2,1,0:T(8,128)(2,1)} %v_ref.1, s32[1,2048]{1,0:T(1,128)} %bitcast.9, s32[64,128]{1,0:T(8,128)} %bitcast.8, bf16[256,512]{1,0:T(8,128)(2,1)} %constant.7.ah_any, bf16[256,512]{1,0:T(8,128)(2,1)} %constant.10.al_any, bf16[512,256]{1,0:T(8,128)(2,1)} %constant.11.ch_any, ...), custom_call_target="tpu_custom_call" | custom-call | tf_op jit(solution)/shard_map/pallas_call | solution.py:395
  100.6 1.9 %shard_map.69 = (f32[1024,128]{1,0:T(8,128)}, f32[256,64]{1,0:T(8,128)}) custom-call(f32[1024,128]{1,0:T(8,128)} %get-tuple-element.6.i_ref, f32[256,64]{1,0:T(8,128)} %get-tuple-element.7.d_ref), custom_call_target="tpu_custom_call" | custom-call | tf_op jit(solution)/shard_map/pallas_call | solution.py:437
